TPU v7x, 32 devices: a whole 2x2x4 slice. The times are simulated.
32 devices in a mesh: dp: 4 (over z), section: 2 (over x), mp: 4 (over y, core).
Axes of the slice: x: 2, y: 2, z: 4, core: 2. Of those that a mesh axis runs over, the one named last changes fastest.
Arguments:
- source_rows: bfloat16 [1024, 1024], P('dp', 'mp'), may hold values from -6 to 6
- value_weight: bfloat16 [2, 1024, 1024], P('section', None, 'mp'), may hold values from -0.1875 to 0.1875
- gate_weight: bfloat16 [2, 1024, 1024], P('section', None, 'mp'), may hold values from -0.1875 to 0.1875
- kernel_weight: bfloat16 [2, 1024, 496], P('section', None, 'mp'), may hold values from -0.1875 to 0.1875
- segment_ids: int32 [8, 128], P('dp'), may hold values from 0 to 3, never falling along the last dimension, each value on 1 to 64 neighbouring positions
- out_grad: bfloat16 [1024, 1024], P('dp', 'mp'), may hold values from -6 to 6
Outputs:
- value_grad: float32 [2, 1024, 1024], P('section', 'dp', 'mp')
- gate_grad: float32 [2, 1024, 1024], P('section', 'dp', 'mp')
- kernel_grad: float32 [2, 1024, 496], P('section', 'dp', 'mp')
Inputs may be any that keep to these rules, and one draw needn't show every extreme that they name: `segment_ids`: in each microbatch row of 128 positions the sentence numbers never fall and every number from 0 up to the largest appears; a sentence covers 1 to 64 positions, and in every microbatch exactly one sentence covers 64 positions.
All inputs are finite; a program needn't handle non-finite values.
Results may differ from a plain program's by a relative error of at most 0.015.
Values may be sent and summed in bfloat16 or wider, within the bound.
A program may use at most 64 MiB of HBM per device.

v0:
```python
import jax
import jax.numpy as jnp
from jax import lax
from jax.sharding import PartitionSpec as P

KERNEL = 31


def from_behind(value, axis, steps):
    count = lax.axis_size(axis)
    initial, last = (max(0, -steps), min(count, count - steps))
    return lax.ppermute(value, axis, [(source, source + steps) for source in range(initial, last)])


def make_table(segments):
    row_count = segments.shape[0]
    positions = jnp.arange(row_count, dtype=jnp.int32)
    offsets = positions[None, :] - positions[:, None] + KERNEL // 2
    same_doc = segments[:, None] == segments[None, :]
    tap_index = jnp.arange(KERNEL, dtype=jnp.int32)[:, None, None]
    return ((offsets[None] == tap_index) & same_doc[None]).astype(jnp.float32)


def normalize(rows_in):
    widened = rows_in.astype(jnp.float32)
    row_mean = jnp.mean(widened, axis=-1, keepdims=True)
    centred = widened - row_mean
    inv_std = lax.rsqrt(jnp.mean(centred * centred, axis=-1, keepdims=True) + 1e-05)
    normed = centred * inv_std
    return (normed, inv_std, normed.astype(jnp.bfloat16))


def forward_pieces(normed_b, band_table, weights):
    w_value, w_gate, w_kernel = weights
    row_count = normed_b.shape[0]
    value_proj = jnp.dot(normed_b, w_value, preferred_element_type=jnp.float32)
    gate_proj = jnp.dot(normed_b, w_gate, preferred_element_type=jnp.float32)
    gate_sig = jax.nn.sigmoid(gate_proj)
    gated = (value_proj * gate_sig).astype(jnp.bfloat16)
    head_count = w_kernel.shape[1] // KERNEL
    head_size = w_value.shape[1] // head_count
    logits = jnp.dot(normed_b, w_kernel, preferred_element_type=jnp.float32).reshape(
        row_count, head_count, KERNEL
    )
    exp_logits = jnp.exp(logits)
    taps = exp_logits / jnp.sum(exp_logits, axis=-1, keepdims=True)
    band_mat = jnp.einsum(
        "thj,jts->hts",
        taps.astype(jnp.bfloat16),
        band_table.astype(jnp.bfloat16),
        preferred_element_type=jnp.float32,
    ).astype(jnp.bfloat16)
    gated3 = gated.reshape(row_count, head_count, head_size)
    mixed = jnp.einsum(
        "hts,shd->thd", band_mat, gated3, preferred_element_type=jnp.float32
    ).reshape(row_count, -1)
    return (value_proj, gate_sig, gated3, taps, band_mat, mixed)


def layer_forward(full_rows, segments, weights, mp_index):
    normed, inv_std, normed_b = normalize(full_rows)
    pieces = forward_pieces(normed_b, make_table(segments), weights)
    half_width = weights[0].shape[1]
    own_part = lax.dynamic_slice_in_dim(
        full_rows.astype(jnp.float32), mp_index * half_width, half_width, 1
    )
    return (own_part + pieces[5]).astype(jnp.bfloat16)


def layer_backward(normed_b, segments, grad_out, weights):
    w_value, w_gate, w_kernel = weights
    band_table = make_table(segments)
    value_proj, gate_sig, gated3, taps, band_mat, mixed = forward_pieces(
        normed_b, band_table, weights
    )
    row_count, head_count, head_size = gated3.shape
    grad_mixed = grad_out.astype(jnp.bfloat16).reshape(row_count, head_count, head_size)
    grad_gated = jnp.einsum(
        "hts,thd->shd", band_mat, grad_mixed, preferred_element_type=jnp.float32
    ).reshape(row_count, -1)
    tap_outer = jnp.einsum("thd,shd->hts", grad_mixed, gated3, preferred_element_type=jnp.float32)
    grad_taps = jnp.einsum("hts,jts->thj", tap_outer, band_table)
    grad_logits = (
        (taps * (grad_taps - jnp.sum(taps * grad_taps, axis=-1, keepdims=True)))
        .astype(jnp.bfloat16)
        .reshape(row_count, -1)
    )
    grad_value = (grad_gated * gate_sig).astype(jnp.bfloat16)
    grad_gate = (grad_gated * value_proj * gate_sig * (1.0 - gate_sig)).astype(jnp.bfloat16)
    dims = (((1,), (1,)), ((), ()))
    grad_part = lax.dot_general(grad_value, w_value, dims, preferred_element_type=jnp.float32)
    grad_part = grad_part + lax.dot_general(
        grad_gate, w_gate, dims, preferred_element_type=jnp.float32
    )
    grad_part = grad_part + lax.dot_general(
        grad_logits, w_kernel, dims, preferred_element_type=jnp.float32
    )
    return (grad_part, jnp.concatenate([grad_value, grad_gate, grad_logits], axis=1))


def shards(source_rows, value_weight, gate_weight, kernel_weight, segment_ids, out_grad):
    section_count = lax.axis_size("section")
    section_index = lax.axis_index("section")
    mp_index = lax.axis_index("mp")
    micro_count, row_count = segment_ids.shape
    full_width = value_weight.shape[1]
    half_width = value_weight.shape[2]
    weights = (value_weight[0], gate_weight[0], kernel_weight[0])
    term_width = 2 * half_width + kernel_weight.shape[2]
    inputs = source_rows.reshape(micro_count, row_count, half_width)
    top_grads = out_grad.reshape(micro_count, row_count, half_width)
    tick_count = micro_count + section_count - 1

    def forward_tick(tick, carry):
        received, stored = carry
        micro_index = tick - section_index
        active = (micro_index >= 0) & (micro_index < micro_count)
        slot_index = jnp.clip(micro_index, 0, micro_count - 1)
        own_rows = jnp.where(section_index == 0, inputs[slot_index], received)
        full_rows = lax.all_gather(own_rows, "mp", axis=1, tiled=True)
        segments = segment_ids[slot_index]
        result = lax.cond(
            active,
            lambda: layer_forward(full_rows, segments, weights, mp_index),
            lambda: jnp.zeros_like(own_rows),
        )
        stored = stored.at[slot_index].set(jnp.where(active, full_rows, stored[slot_index]))
        passed = from_behind(result, "section", 1)
        return (passed, stored)

    start_rows = jnp.zeros((row_count, half_width), jnp.bfloat16)
    start_store = jnp.zeros((micro_count, row_count, full_width), jnp.bfloat16)
    unused, stored = lax.fori_loop(0, tick_count, forward_tick, (start_rows, start_store))

    def backward_tick(tick, carry):
        received, grads, terms_store = carry
        micro_index = tick - (section_count - 1 - section_index)
        active = (micro_index >= 0) & (micro_index < micro_count)
        slot_index = jnp.clip(micro_index, 0, micro_count - 1)
        top_grad = top_grads[slot_index].astype(jnp.float32)
        grad_out = jnp.where(section_index == section_count - 1, top_grad, received)
        segments = segment_ids[slot_index]
        normed, inv_std, normed_b = normalize(stored[slot_index])
        grad_part, grad_terms = lax.cond(
            active,
            lambda: layer_backward(normed_b, segments, grad_out, weights),
            lambda: (
                jnp.zeros((row_count, full_width), jnp.float32),
                jnp.zeros((row_count, term_width), jnp.bfloat16),
            ),
        )
        grad_normed = lax.psum(grad_part.astype(jnp.bfloat16), "mp").astype(jnp.float32)
        norm_back = inv_std * (
            grad_normed
            - jnp.mean(grad_normed, axis=-1, keepdims=True)
            - normed * jnp.mean(grad_normed * normed, axis=-1, keepdims=True)
        )
        own_back = lax.dynamic_slice_in_dim(norm_back, mp_index * half_width, half_width, 1)
        grad_in = grad_out + own_back
        grad_in = jnp.where(active, grad_in, 0.0)
        grads = lax.cond(
            active,
            lambda: grads
            + lax.dot_general(
                normed_b, grad_terms, (((0,), (0,)), ((), ())), preferred_element_type=jnp.float32
            ),
            lambda: grads,
        )
        passed = from_behind(grad_in.astype(jnp.bfloat16), "section", -1).astype(grad_in.dtype)
        return (passed, grads, terms_store)

    start_grads = jnp.zeros((full_width, term_width), jnp.float32)
    start_terms = jnp.zeros((1,), jnp.bfloat16)
    start_back = jnp.zeros((row_count, half_width), jnp.float32)
    unused, grads, terms_store = lax.fori_loop(
        0, tick_count, backward_tick, (start_back, start_grads, start_terms)
    )
    shares = lax.psum_scatter(
        grads.astype(jnp.bfloat16), "dp", scatter_dimension=0, tiled=True
    ).astype(jnp.float32)
    value_share = shares[:, :half_width][None]
    gate_share = shares[:, half_width : 2 * half_width][None]
    kernel_share = shares[:, 2 * half_width :][None]
    return (value_share, gate_share, kernel_share)


def solution(mesh):
    in_specs = (
        P("dp", "mp"),
        P("section", None, "mp"),
        P("section", None, "mp"),
        P("section", None, "mp"),
        P("dp", None),
        P("dp", "mp"),
    )
    out_specs = (P("section", "dp", "mp"), P("section", "dp", "mp"), P("section", "dp", "mp"))
    return jax.shard_map(shards, mesh=mesh, in_specs=in_specs, out_specs=out_specs, check_vma=False)
```

profile of v0, /device:TPU:0, one launch (start us, length us, event | category | flops | bytes accessed | tf_op | source)
XLA Modules:
  0.0 359.8 jit_solution(7524102810339772016)
XLA Ops:
  8.1 50.1 %while.38 = (s32[]{:T(128)}, bf16[128,256]{0,1:T(8,128)(2,1)S(1)}, bf16[2,128,1024]{1,2,0:T(8,128)(2,1)S(1)}, s32[]{:T(128)}, pred[]{:T(512)}, /*index=5*/bf16[2...) while((s32[]{:T(128)}, bf16[128,256]{0,1:T(8,128)(2,1)S(1)}, ...), condition=%wide.region_7.8_spmd, body=%wide.region_0.7_spmd.sunk | while | flops 184383632 | bytes 11819549 | solution.py:133
  9.1 7.2 %all_gather.9 = bf16[128,1024]{0,1:T(8,128)(2,1)S(1)} all-gather(bf16[128,256]{0,1:T(8,128)(2,1)S(1)} %bitcast_select_fusion.4), channel_id=1, replica_groups=mesh['dp'=4,'section'=2,'mp'=4] {'mp'}, dimensions={1}, use_global_device_ids=true | all-gather | bytes 327680 | tf_op jit(solution)/shard_map/while/body/eval_jaxpr/all_gather | solution.py:120
  16.4 4.1 %conditional.8 = (bf16[128,256]{0,1:T(8,128)(2,1)S(1)}) conditional(s32[]{:T(128)} %convert_element_type.241, () %tuple.133, (bf16[128,1024]{0,1:T(8,128)(2,1)S(1)}, s32[]{:T(128)}, bf16[1024,256]{1,0:T(8,128)(2,1)}, bf16[1024,256]{1,0:T(8,128)(2,1)}, s32[2,128]{1,0:T(2,128)}, /*index=5*/s32[]{:T(128)}, bf16[1024,124]{1,0:T(8,128)(2,1)}) %tuple.134), branch_computations={%region_1.1_spmd, %region_2.5_spmd} | conditional | flops 184088704 | bytes 9459834 | solution.py:122
  24.9 5.8 %all_gather.9 = bf16[128,1024]{0,1:T(8,128)(2,1)S(1)} all-gather(bf16[128,256]{0,1:T(8,128)(2,1)S(1)} %bitcast_select_fusion.4), channel_id=1, replica_groups=mesh['dp'=4,'section'=2,'mp'=4] {'mp'}, dimensions={1}, use_global_device_ids=true | all-gather | bytes 327680 | tf_op jit(solution)/shard_map/while/body/eval_jaxpr/all_gather | solution.py:120
  30.7 4.1 %conditional.8 = (bf16[128,256]{0,1:T(8,128)(2,1)S(1)}) conditional(s32[]{:T(128)} %convert_element_type.241, () %tuple.133, (bf16[128,1024]{0,1:T(8,128)(2,1)S(1)}, s32[]{:T(128)}, bf16[1024,256]{1,0:T(8,128)(2,1)}, bf16[1024,256]{1,0:T(8,128)(2,1)}, s32[2,128]{1,0:T(2,128)}, /*index=5*/s32[]{:T(128)}, bf16[1024,124]{1,0:T(8,128)(2,1)}) %tuple.134), branch_computations={%region_1.1_spmd, %region_2.5_spmd} | conditional | flops 184088704 | bytes 9459834 | solution.py:122
  34.8 4.4 %collective-permute-start = (bf16[128,256]{0,1:T(8,128)(2,1)S(1)}, bf16[128,256]{0,1:T(8,128)(2,1)S(1)}, u32[]{:S(2)}, u32[]{:S(2)}) collective-permute-start(bf16[128,256]{0,1:T(8,128)(2,1)S(1)} %get-tuple-element.1041), channel_id=1, source_target_pairs={{0,4},{1,5},{2,6},{3,7},{8,12},{9,13},{10,14},{11,15},{16,20},{17,... | collective-permute-start | bytes 196616 | tf_op jit(solution)/shard_map/while/body/eval_jaxpr/ppermute | solution.py:12
  42.1 5.8 %all_gather.9 = bf16[128,1024]{0,1:T(8,128)(2,1)S(1)} all-gather(bf16[128,256]{0,1:T(8,128)(2,1)S(1)} %bitcast_select_fusion.4), channel_id=1, replica_groups=mesh['dp'=4,'section'=2,'mp'=4] {'mp'}, dimensions={1}, use_global_device_ids=true | all-gather | bytes 327680 | tf_op jit(solution)/shard_map/while/body/eval_jaxpr/all_gather | solution.py:120
  47.9 8.5 %collective-permute-start = (bf16[128,256]{0,1:T(8,128)(2,1)S(1)}, bf16[128,256]{0,1:T(8,128)(2,1)S(1)}, u32[]{:S(2)}, u32[]{:S(2)}) collective-permute-start(bf16[128,256]{0,1:T(8,128)(2,1)S(1)} %get-tuple-element.1041), channel_id=1, source_target_pairs={{0,4},{1,5},{2,6},{3,7},{8,12},{9,13},{10,14},{11,15},{16,20},{17,... | collective-permute-start | bytes 196616 | tf_op jit(solution)/shard_map/while/body/eval_jaxpr/ppermute | solution.py:12
  59.5 257.4 %while.39 = (s32[]{:T(128)}, f32[128,256]{1,0:T(8,128)}, f32[1024,636]{1,0:T(8,128)S(1)}, s32[]{:T(128)}, pred[]{:T(512)}, /*index=5*/bf16[2,128,256]{2,1,0:T(8,...) while((s32[]{:T(128)}, f32[128,256]{1,0:T(8,128)}, ...), condition=%wide.region_20.21_spmd.clone, body=%wide.region_8.20_spmd.clone.sunk | while | flops 533156512 | bytes 23325744 | solution.py:175
  65.9 71.7 %all-reduce.2.cloned.1.call-done = bf16[128,1024]{1,0:T(8,128)(2,1)} async-done(((bf16[128,1024]{1,0:T(8,128)(2,1)}), bf16[128,1024]{1,0:T(8,128)(2,1)}) %all-reduce.2.cloned.1.call-update) | async-done | bytes 262160 | tf_op jit(solution)/shard_map/while/body/eval_jaxpr/psum | solution.py:152
  141.8 4.8 %collective-permute-done.1 = bf16[128,256]{1,0:T(8,128)(2,1)S(1)} collective-permute-done((bf16[128,256]{1,0:T(8,128)(2,1)S(1)}, bf16[128,256]{1,0:T(8,128)(2,1)S(1)}, u32[]{:S(2)}, u32[]{:S(2)}) %collective-permute-start.1) | collective-permute-done | bytes 65568 | tf_op jit(solution)/shard_map/while/body/eval_jaxpr/ppermute | solution.py:12
  152.3 38.8 %conditional.9 = (bf16[128,1024]{1,0:T(8,128)(2,1)}, bf16[128,636]{1,0:T(8,128)(2,1)}) conditional(s32[]{:T(128)} %convert_element_type.248, () %tuple.138, (s32[2,128]{1,0:T(2,128)}, s32[]{:T(128)}, bf16[128,1024]{1,0:T(8,128)(2,1)}, bf16[1024,124]{1,0:T(8,128)(2,1)}, f32[128,256]{1,0:T(8,128)S(1)}, /*index=5*/bf16[1024,256]{1,0:T(8,128)(2,1)}, ...), branch_computations={%region_11.11_spmd, %region_12.14_spmd} | conditional | flops 362930720 | bytes 10925676 | solution.py:144
  160.7 2.0 fusion.23
  168.4 2.0 multiply_convert_fusion.4
  176.9 7.4 %fusion.20 = bf16[128,4,31]{2,1,0:T(4,128)(2,1)} fusion(f32[128,4,31]{2,1,0:T(4,128)S(1)} %fusion.16, f32[128,4,31]{2,1,0:T(4,128)} %copy.31, f32[128,4]{1,0:T(8,128)} %copy.30), kind=kOutput, calls=%fused_computation.45 | output fusion | flops 95774 | bytes 160768 | tf_op jit(solution)/shard_map/while/body/eval_jaxpr/cond/branch_1_fun/sub | solution.py:84
  191.1 31.2 %all-reduce.2.cloned.1.call-done = bf16[128,1024]{1,0:T(8,128)(2,1)} async-done(((bf16[128,1024]{1,0:T(8,128)(2,1)}), bf16[128,1024]{1,0:T(8,128)(2,1)}) %all-reduce.2.cloned.1.call-update) | async-done | bytes 262160 | tf_op jit(solution)/shard_map/while/body/eval_jaxpr/psum | solution.py:152
  228.3 3.1 collective-permute-done.1
  237.1 38.8 %conditional.9 = (bf16[128,1024]{1,0:T(8,128)(2,1)}, bf16[128,636]{1,0:T(8,128)(2,1)}) conditional(s32[]{:T(128)} %convert_element_type.248, () %tuple.138, (s32[2,128]{1,0:T(2,128)}, s32[]{:T(128)}, bf16[128,1024]{1,0:T(8,128)(2,1)}, bf16[1024,124]{1,0:T(8,128)(2,1)}, f32[128,256]{1,0:T(8,128)S(1)}, /*index=5*/bf16[1024,256]{1,0:T(8,128)(2,1)}, ...), branch_computations={%region_11.11_spmd, %region_12.14_spmd} | conditional | flops 362930720 | bytes 10925676 | solution.py:144
  245.5 2.0 fusion.23
  253.2 2.0 multiply_convert_fusion.4
  261.7 7.4 %fusion.20 = bf16[128,4,31]{2,1,0:T(4,128)(2,1)} fusion(f32[128,4,31]{2,1,0:T(4,128)S(1)} %fusion.16, f32[128,4,31]{2,1,0:T(4,128)} %copy.31, f32[128,4]{1,0:T(8,128)} %copy.30), kind=kOutput, calls=%fused_computation.45 | output fusion | flops 95774 | bytes 160768 | tf_op jit(solution)/shard_map/while/body/eval_jaxpr/cond/branch_1_fun/sub | solution.py:84
  275.9 31.2 %all-reduce.2.cloned.1.call-done = bf16[128,1024]{1,0:T(8,128)(2,1)} async-done(((bf16[128,1024]{1,0:T(8,128)(2,1)}), bf16[128,1024]{1,0:T(8,128)(2,1)}) %all-reduce.2.cloned.1.call-update) | async-done | bytes 262160 | tf_op jit(solution)/shard_map/while/body/eval_jaxpr/psum | solution.py:152
  313.1 3.1 collective-permute-done.1
  318.2 31.9 %reduce-scatter.2.cloned.1.call-done = bf16[256,636]{1,0:T(8,128)(2,1)} async-done(((bf16[1024,636]{1,0:T(8,128)(2,1)}), bf16[256,636]{1,0:T(8,128)(2,1)}) %reduce-scatter.2.cloned.1.call-update) | async-done | bytes 325648 | tf_op jit(solution)/shard_map/reduce_scatter | solution.py:178
  (213 shorter events, 117.2 us)
Async XLA Ops:
  16.4 5.5 %copy-start.9 = (s32[3]{0:T(128)S(1)}, s32[3]{0:T(128)}, u32[]{:S(2)}) copy-start(s32[3]{0:T(128)} %get-tuple-element.994) | copy-start | bytes 40 | tf_op jit(solution)/shard_map/while
  16.4 3.2 copy-start
  16.4 3.4 copy-start.5
  20.5 3.4 collective-permute-start
  30.7 8.6 %copy-start.9 = (s32[3]{0:T(128)S(1)}, s32[3]{0:T(128)}, u32[]{:S(2)}) copy-start(s32[3]{0:T(128)} %get-tuple-element.994) | copy-start | bytes 40 | tf_op jit(solution)/shard_map/while
  30.7 3.2 copy-start
  30.7 3.4 copy-start.5
  34.8 6.3 %collective-permute-start = (bf16[128,256]{0,1:T(8,128)(2,1)S(1)}, bf16[128,256]{0,1:T(8,128)(2,1)S(1)}, u32[]{:S(2)}, u32[]{:S(2)}) collective-permute-start(bf16[128,256]{0,1:T(8,128)(2,1)S(1)} %get-tuple-element.1041), channel_id=1, source_target_pairs={{0,4},{1,5},{2,6},{3,7},{8,12},{9,13},{10,14},{11,15},{16,20},{17,... | collective-permute-start | bytes 196616 | tf_op jit(solution)/shard_map/while/body/eval_jaxpr/ppermute | solution.py:12
  47.9 8.5 %copy-start.9 = (s32[3]{0:T(128)S(1)}, s32[3]{0:T(128)}, u32[]{:S(2)}) copy-start(s32[3]{0:T(128)} %get-tuple-element.994) | copy-start | bytes 40 | tf_op jit(solution)/shard_map/while
  47.9 10.4 %collective-permute-start = (bf16[128,256]{0,1:T(8,128)(2,1)S(1)}, bf16[128,256]{0,1:T(8,128)(2,1)S(1)}, u32[]{:S(2)}, u32[]{:S(2)}) collective-permute-start(bf16[128,256]{0,1:T(8,128)(2,1)S(1)} %get-tuple-element.1041), channel_id=1, source_target_pairs={{0,4},{1,5},{2,6},{3,7},{8,12},{9,13},{10,14},{11,15},{16,20},{17,... | collective-permute-start | bytes 196616 | tf_op jit(solution)/shard_map/while/body/eval_jaxpr/ppermute | solution.py:12
  58.3 1.2 copy-start.1
  59.5 78.1 %all-reduce.2.cloned.1.call-start = ((), (), s32[]{:S(2)}) async-start(), calls=%async_computation.2 | async-start | bytes 524288 | tf_op jit(solution)/shard_map/while/body/eval_jaxpr/psum | solution.py:152
  140.5 6.2 %collective-permute-start.1 = (bf16[128,256]{1,0:T(8,128)(2,1)S(1)}, bf16[128,256]{1,0:T(8,128)(2,1)S(1)}, u32[]{:S(2)}, u32[]{:S(2)}) collective-permute-start(bf16[128,256]{1,0:T(8,128)(2,1)S(1)} %fusion.74), channel_id=1, source_target_pairs={{4,0},{5,1},{6,2},{7,3},{12,8},{13,9},{14,10},{15,11},{20,16},{21,... | collective-permute-start | bytes 196616 | tf_op jit(solution)/shard_map/while/body/eval_jaxpr/ppermute | solution.py:12
  147.3 75.0 %all-reduce.2.cloned.1.call-start = ((), (), s32[]{:S(2)}) async-start(), calls=%async_computation.2 | async-start | bytes 524288 | tf_op jit(solution)/shard_map/while/body/eval_jaxpr/psum | solution.py:152
  164.4 1.5 copy-start.4
  186.0 4.2 %copy-start.2 = (bf16[1024,124]{1,0:T(8,128)(2,1)S(1)}, bf16[1024,124]{1,0:T(8,128)(2,1)}, u32[]{:S(2)}) copy-start(bf16[1024,124]{1,0:T(8,128)(2,1)} %get-tuple-element.579) | copy-start | bytes 761860 | tf_op jit(solution)/shard_map/while/body/eval_jaxpr/cond
  186.0 4.2 %copy-start.6 = (bf16[128,124]{1,0:T(8,128)(2,1)S(1)}, bf16[128,124]{1,0:T(8,128)(2,1)}, u32[]{:S(2)}) copy-start(bf16[128,124]{1,0:T(8,128)(2,1)} %reshape.248) | copy-start | bytes 95236 | tf_op jit(solution)/shard_map/while/body/eval_jaxpr/cond
  225.3 6.2 %collective-permute-start.1 = (bf16[128,256]{1,0:T(8,128)(2,1)S(1)}, bf16[128,256]{1,0:T(8,128)(2,1)S(1)}, u32[]{:S(2)}, u32[]{:S(2)}) collective-permute-start(bf16[128,256]{1,0:T(8,128)(2,1)S(1)} %fusion.74), channel_id=1, source_target_pairs={{4,0},{5,1},{6,2},{7,3},{12,8},{13,9},{14,10},{15,11},{20,16},{21,... | collective-permute-start | bytes 196616 | tf_op jit(solution)/shard_map/while/body/eval_jaxpr/ppermute | solution.py:12
  232.1 75.0 %all-reduce.2.cloned.1.call-start = ((), (), s32[]{:S(2)}) async-start(), calls=%async_computation.2 | async-start | bytes 524288 | tf_op jit(solution)/shard_map/while/body/eval_jaxpr/psum | solution.py:152
  249.2 1.5 copy-start.4
  270.8 4.2 %copy-start.2 = (bf16[1024,124]{1,0:T(8,128)(2,1)S(1)}, bf16[1024,124]{1,0:T(8,128)(2,1)}, u32[]{:S(2)}) copy-start(bf16[1024,124]{1,0:T(8,128)(2,1)} %get-tuple-element.579) | copy-start | bytes 761860 | tf_op jit(solution)/shard_map/while/body/eval_jaxpr/cond
  270.8 4.2 %copy-start.6 = (bf16[128,124]{1,0:T(8,128)(2,1)S(1)}, bf16[128,124]{1,0:T(8,128)(2,1)}, u32[]{:S(2)}) copy-start(bf16[128,124]{1,0:T(8,128)(2,1)} %reshape.248) | copy-start | bytes 95236 | tf_op jit(solution)/shard_map/while/body/eval_jaxpr/cond
  310.1 6.2 %collective-permute-start.1 = (bf16[128,256]{1,0:T(8,128)(2,1)S(1)}, bf16[128,256]{1,0:T(8,128)(2,1)S(1)}, u32[]{:S(2)}, u32[]{:S(2)}) collective-permute-start(bf16[128,256]{1,0:T(8,128)(2,1)S(1)} %fusion.74), channel_id=1, source_target_pairs={{4,0},{5,1},{6,2},{7,3},{12,8},{13,9},{14,10},{15,11},{20,16},{21,... | collective-permute-start | bytes 196616 | tf_op jit(solution)/shard_map/while/body/eval_jaxpr/ppermute | solution.py:12
  316.9 33.1 %reduce-scatter.2.cloned.1.call-start = ((), (), s32[]{:S(2)}) async-start(), calls=%async_computation.1 | async-start | bytes 1638400 | tf_op jit(solution)/shard_map/reduce_scatter | solution.py:178
  (7 other events, 7.0 us)
Sparse Core Ops, SparseCore 0:
  66.0 71.5 all-reduce.1
  191.3 31.0 all-reduce.1
  276.0 31.0 all-reduce.1
Sparse Core Ops, SparseCore 1:
  319.7 30.3 reduce-scatter.1
where the time goes:
time: 362 us; the launch traced here: 360 us
  waiting for transfers between devices  179 us (49%)
  other arithmetic  47.1 us (13%)
  local copies, waits for them, and re-layouts  42.7 us (12%)
  matrix products  38.4 us (11%)
  blocking collectives  18.8 us (5%)
  starting transfers between devices  18 us (5%)
  between operations  15.2 us (4%)
    psum x3, waiting for transfers between devices, backward_tick(): lax.psum(grad_part.astype(jnp.bfloat16), 'mp').astype(jnp.float32)  134 us
    reduce_scatter x1, waiting for transfers between devices, shards(): lax.psum_scatter(grads.astype(jnp.bfloat16), 'dp', scatter_dimension=0, t...  31.9 us
    all_gather x3, blocking collectives, forward_tick(): full_rows = lax.all_gather(own_rows, 'mp', axis=1, tiled=True)  18.8 us
    ppermute x6, starting transfers between devices, from_behind(): lax.ppermute(value, axis, [(source, source + steps) for source in range(i...  18 us
    sub x2, other arithmetic, layer_backward(): grad_taps - jnp.sum(taps * grad_taps, axis=-1, keepdims=True)  14.8 us
    ppermute x6, waiting for transfers between devices, from_behind(): lax.ppermute(value, axis, [(source, source + steps) for source in range(i...  12.7 us
    dynamic_slice x6, local copies, waits for them, and re-layouts, backward_tick(): normed, inv_std, normed_b = normalize(stored[slot_index])  8.26 us
  transfers between devices with their start and end apart: 10, of which 10 were waited for; matrix products, arithmetic and copies ran while one was open for 2% of the time, Pallas kernels for 0%

commit v1 on v0

v1 whole, which is shorter than its diff:
```python
import functools

import jax
import jax.numpy as jnp
from jax import lax
from jax.experimental import pallas as pl
from jax.experimental.pallas import tpu as pltpu
from jax.sharding import PartitionSpec as P

KERNEL = 31
MESH = pl.DeviceIdType.MESH
F32 = jnp.float32
BF16 = jnp.bfloat16


def remote(src, dst, send_sem, recv_sem, device):
    return pltpu.make_async_remote_copy(
        src_ref=src,
        dst_ref=dst,
        send_sem=send_sem,
        recv_sem=recv_sem,
        device_id=device,
        device_id_type=MESH,
    )


def dot(a, b):
    return jnp.dot(a, b, preferred_element_type=F32)


def dot_nt(a, b):
    return lax.dot_general(a, b, (((1,), (1,)), ((), ())), preferred_element_type=F32)


def dot_tn(a, b):
    return lax.dot_general(a, b, (((0,), (0,)), ((), ())), preferred_element_type=F32)


def skew(values, shift):
    fine = shift % 8
    if fine:
        values = pltpu.roll(values, fine, 1)
    return pltpu.roll(values, shift - fine, 1, stride=1, stride_axis=0)


def kernel(
    n_dp,
    micro,
    src_ref,
    wv_ref,
    wg_ref,
    wk_ref,
    seg_ref,
    og_ref,
    vout_ref,
    gout_ref,
    kout_ref,
    xall,
    nf,
    nb,
    invs,
    nt_full,
    nt_all,
    wkp,
    lgs,
    masks,
    vs,
    sigs,
    gateds,
    tps,
    bds,
    hs,
    gbuf,
    gs,
    terms,
    rs_buf,
    rs_in,
    st_buf,
    st_in,
    acc,
    ag_send,
    ag_recv,
    h_send,
    h_recv,
    nt_send,
    nt_recv,
    right_send,
    left_send,
    ring_recv,
    rs_send,
    rs_recv,
    st_send,
    st_recv,
    g_send,
    g_recv,
):
    d = lax.axis_index("dp")
    s = lax.axis_index("section")
    m = lax.axis_index("mp")
    near = m + 1 - 2 * lax.rem(m, 2)
    across = lax.rem(m + 2, 4)
    corner = lax.rem(near + 2, 4)
    partners = (near, across, corner)
    other = {"section": 1 - s}
    rows = seg_ref.shape[1]
    width = wv_ref.shape[2]
    full = wv_ref.shape[1]
    kcols = wk_ref.shape[2]
    heads = kcols // KERNEL
    n_mp = full // width
    slab = full // n_dp
    micros = range(micro)

    lanes = lax.broadcasted_iota(jnp.int32, (rows, rows), 1)
    subs = lax.broadcasted_iota(jnp.int32, (rows, rows), 0)
    offset = lanes - subs + KERNEL // 2
    cyclic = lax.rem(offset + rows, rows) < KERNEL
    low_half = lanes < rows // 2
    flip = jnp.where(lanes + subs == rows - 1, 1.0, 0.0).astype(BF16)

    barrier = pltpu.get_barrier_semaphore()
    for p in partners:
        pl.semaphore_signal(barrier, inc=1, device_id={"mp": p}, device_id_type=MESH)
    pl.semaphore_signal(barrier, inc=1, device_id=other, device_id_type=MESH)

    def greet(i, carry):
        pl.semaphore_signal(
            barrier, inc=1, device_id={"dp": lax.rem(d + i, n_dp)}, device_id_type=MESH
        )
        return carry

    lax.fori_loop(1, n_dp, greet, 0)

    @pl.when(s == 0)
    def _():
        for mb in micros:
            xall[mb, m] = src_ref[mb * rows : (mb + 1) * rows, :]

    @pl.when(s == 1)
    def _():
        for mb in micros:
            gbuf[mb] = og_ref[mb * rows : (mb + 1) * rows, :]

    pl.semaphore_wait(barrier, 4 + n_dp - 1)

    def gather_copy(mb, rel):
        block = (m, m, across)[rel]
        target = (near, across, near)[rel]
        return remote(
            xall.at[mb, block],
            xall.at[mb, block],
            ag_send.at[mb, rel],
            ag_recv.at[mb, rel],
            {"mp": target},
        )

    def gather_wait(mb, rel):
        block = (near, across, corner)[rel]
        remote(
            xall.at[mb, block],
            xall.at[mb, block],
            ag_send.at[mb, rel],
            ag_recv.at[mb, rel],
            {"mp": near},
        ).wait_recv()

    def h_copy(mb):
        return remote(hs.at[mb], xall.at[mb, m], h_send.at[mb], h_recv.at[mb], other)

    def g_copy(mb):
        return remote(gs.at[mb], gbuf.at[mb], g_send.at[mb], g_recv.at[mb], other)

    @pl.when(s == 0)
    def _():
        for mb in micros:
            gather_copy(mb, 1).start()
            gather_copy(mb, 0).start()

    wkp[...] = jnp.zeros_like(wkp)
    wkp[:, :kcols] = wk_ref[0]
    lgs[...] = jnp.zeros_like(lgs)
    acc[...] = jnp.zeros_like(acc)
    for mb in micros:
        across_seg = jnp.broadcast_to(seg_ref[mb : mb + 1, :].astype(F32), (rows, rows))
        down_seg = jnp.transpose(across_seg)
        same = (across_seg == down_seg) & (offset >= 0) & (offset < KERNEL)
        masks[mb] = jnp.where(same, 1.0, 0.0)

    def forward(mb):
        @pl.when(s == 1)
        def _():
            h_copy(mb).wait_recv()
            gather_copy(mb, 1).start()
            gather_copy(mb, 0).start()

        gather_wait(mb, 1)
        gather_copy(mb, 2).start()
        gather_wait(mb, 0)
        gather_wait(mb, 2)
        blocks = [xall[mb, j].astype(F32) for j in range(n_mp)]
        mean = sum(jnp.sum(b, axis=1, keepdims=True) for b in blocks) / full
        centred = [b - mean for b in blocks]
        var = sum(jnp.sum(c * c, axis=1, keepdims=True) for c in centred) / full
        inv = lax.rsqrt(var + 1e-05)
        invs[mb] = jnp.broadcast_to(inv, (rows, rows))
        for j in range(n_mp):
            normed = centred[j] * inv
            nf[mb, j] = normed
            nb[mb, :, j * width : (j + 1) * width] = normed.astype(BF16)
        normed_b = nb[mb]
        lgs[...] = dot(normed_b, wkp[...])
        value = dot(normed_b, wv_ref[0])
        sig = jax.nn.sigmoid(dot(normed_b, wg_ref[0]))
        vs[mb] = value
        sigs[mb] = sig
        gateds[mb] = (value * sig).astype(BF16)
        logits = lgs[...]
        in_band = masks[mb] > 0.0
        for h in range(heads):
            shift = (rows - KERNEL // 2 - KERNEL * h) % rows
            skewed = skew(logits, shift)
            weights = jnp.where(cyclic, jnp.exp(skewed), 0.0)
            taps = weights / jnp.sum(weights, axis=1, keepdims=True)
            tps[mb, h] = taps
            bds[mb, h] = jnp.where(in_band, taps, 0.0).astype(BF16)

        @pl.when(s == 0)
        def _():
            for p in range(heads // 2):
                cols = slice(p * rows, (p + 1) * rows)
                pair = gateds[mb, :, cols]
                mixed = jnp.where(
                    low_half, dot(bds[mb, 2 * p], pair), dot(bds[mb, 2 * p + 1], pair)
                )
                own = src_ref[mb * rows : (mb + 1) * rows, cols].astype(F32)
                hs[mb, :, cols] = (own + mixed).astype(BF16)
            h_copy(mb).start()

        for j in range(n_mp):
            nt_full[mb, j * width : (j + 1) * width, :] = jnp.transpose(nf[mb, j]).astype(BF16)

        def share(i, carry):
            k = lax.rem(d + i, n_dp)
            nt_copy(mb, k).start()
            return carry

        lax.fori_loop(1, n_dp, share, 0)
        nt_all[mb, d] = nt_full[mb, pl.ds(pl.multiple_of(d * slab, slab), slab), :]

    def nt_copy(mb, k):
        return remote(
            nt_full.at[mb, pl.ds(pl.multiple_of(k * slab, slab), slab), :],
            nt_all.at[mb, d],
            nt_send.at[mb, k],
            nt_recv.at[mb, d],
            {"dp": k},
        )

    def ring_copy(mb, k, step):
        sems = right_send if step == 1 else left_send
        return remote(
            terms.at[mb, k],
            terms.at[mb, k],
            sems.at[mb, k],
            ring_recv.at[mb, k],
            {"dp": d + step},
        )

    def ring_start(mb, k_right, k_left):
        @pl.when((d + 1 < n_dp) & (k_right >= 0))
        def _():
            ring_copy(mb, k_right, 1).start()

        @pl.when((d > 0) & (k_left < n_dp))
        def _():
            ring_copy(mb, k_left, -1).start()

    def backward(mb):
        @pl.when(s == 0)
        def _():
            g_copy(mb).wait_recv()

        in_band = masks[mb] > 0.0
        grad_logits = jnp.zeros((rows, rows), F32)
        for p in range(heads // 2):
            cols = slice(p * rows, (p + 1) * rows)
            grad_pair = gbuf[mb, :, cols]
            gated_pair = gateds[mb, :, cols]
            grad_gated = jnp.where(
                low_half,
                dot_tn(bds[mb, 2 * p], grad_pair),
                dot_tn(bds[mb, 2 * p + 1], grad_pair),
            )
            sig = sigs[mb, :, cols]
            grad_value = grad_gated * sig
            terms[mb, d, :, cols] = grad_value.astype(BF16)
            grad_gate = grad_value * vs[mb, :, cols] * (1.0 - sig)
            terms[mb, d, :, width + p * rows : width + (p + 1) * rows] = grad_gate.astype(BF16)
            for half in range(2):
                h = 2 * p + half
                keep = low_half if half == 0 else ~low_half
                part = jnp.where(keep, grad_pair.astype(F32), 0.0).astype(BF16)
                grad_taps = jnp.where(in_band, dot_nt(part, gated_pair), 0.0)
                taps = tps[mb, h]
                inner = jnp.sum(taps * grad_taps, axis=1, keepdims=True)
                skewed = (taps * (grad_taps - inner)).astype(BF16)
                shift = (KERNEL // 2 + KERNEL * h + 1) % rows
                grad_logits = grad_logits + skew(dot(flip, skewed), shift)
        terms[mb, d, :, 2 * width :] = dot(flip, grad_logits.astype(BF16)).astype(BF16)

        @pl.when(s == 0)
        def _():
            ring_start(mb, d, d)

        @pl.when(s == 1)
        def _():
            grad_value = terms[mb, d, :, :width]
            grad_gate = terms[mb, d, :, width : 2 * width]
            grad_log = terms[mb, d, :, 2 * width :]
            first = jnp.zeros((rows, 1), F32)
            second = jnp.zeros((rows, 1), F32)
            for j in range(n_mp):
                span = slice(j * width, (j + 1) * width)
                part = dot_nt(grad_value, wv_ref[0, span, :])
                part = part + dot_nt(grad_gate, wg_ref[0, span, :])
                part = part + dot_nt(grad_log, wkp[span, :])
                rs_buf[mb, j] = part.astype(BF16)
                first = first + jnp.sum(part, axis=1, keepdims=True)
                second = second + jnp.sum(part * nf[mb, j], axis=1, keepdims=True)
            both = jnp.transpose(jnp.where(lanes == 0, first, second))
            st_buf[mb] = both[:8]
            for rel in range(3):
                rs_copy(mb, rel).start()
                st_copy(mb, rel).start()
            ring_start(mb, d, d)

    def rs_copy(mb, rel):
        return remote(
            rs_buf.at[mb, partners[rel]],
            rs_in.at[mb, rel],
            rs_send.at[mb, rel],
            rs_recv.at[mb, rel],
            {"mp": partners[rel]},
        )

    def st_copy(mb, rel):
        return remote(
            st_buf.at[mb],
            st_in.at[mb, rel],
            st_send.at[mb, rel],
            st_recv.at[mb, rel],
            {"mp": partners[rel]},
        )

    def finish(mb):
        total = rs_buf[mb, m].astype(F32)
        stats = st_buf[mb]
        for rel in range(3):
            rs_copy(mb, rel).wait_recv()
            st_copy(mb, rel).wait_recv()
            total = total + rs_in[mb, rel].astype(F32)
            stats = stats + st_in[mb, rel]
        columns = jnp.transpose(stats) / full
        inv = invs[mb][:, :1]
        grad = inv * (total - columns[:, 0:1] - nf[mb, m] * columns[:, 1:2])
        gs[mb] = (gbuf[mb].astype(F32) + grad).astype(BF16)
        g_copy(mb).start()

    for mb in micros:
        forward(mb)
    for mb in micros:
        backward(mb)

        @pl.when(s == 1)
        def _():
            finish(mb)

    def accumulate(mb, k):
        acc[...] += dot(nt_all[mb, k], terms[mb, k])

    for mb in micros:
        accumulate(mb, d)

    def ring_step(i, carry):
        for mb in micros:
            left, right = d - i, d + i

            @pl.when(left >= 0)
            def _():
                ring_copy(mb, left, -1).wait_recv()

            @pl.when(right < n_dp)
            def _():
                ring_copy(mb, right, 1).wait_recv()

            ring_start(mb, left, right)
            for k, there in ((left, left >= 0), (right, right < n_dp)):

                @pl.when(there)
                def _():
                    remote(
                        nt_all.at[mb, k],
                        nt_all.at[mb, k],
                        nt_send.at[mb, k],
                        nt_recv.at[mb, k],
                        {"dp": k},
                    ).wait_recv()
                    accumulate(mb, k)

        return carry

    lax.fori_loop(1, n_dp, ring_step, 0)

    vout_ref[0] = acc[:, :width]
    gout_ref[0] = acc[:, width : 2 * width]
    kout_ref[0] = acc[:, 2 * width : 2 * width + kcols]

    for mb in micros:
        for rel in range(3):
            gather_copy(mb, rel).wait_send()

        @pl.when(s == 0)
        def _():
            h_copy(mb).wait_send()

        @pl.when(s == 1)
        def _():
            g_copy(mb).wait_send()
            for rel in range(3):
                rs_copy(mb, rel).wait_send()
                st_copy(mb, rel).wait_send()

        def drain(i, carry):
            @pl.when(i > 0)
            def _():
                nt_copy(mb, lax.rem(d + i, n_dp)).wait_send()

            @pl.when((d + 1 < n_dp) & (d - i >= 0))
            def _():
                ring_copy(mb, d - i, 1).wait_send()

            @pl.when((d > 0) & (d + i < n_dp))
            def _():
                ring_copy(mb, d + i, -1).wait_send()

            return carry

        lax.fori_loop(0, n_dp, drain, 0)


def shards(source_rows, value_weight, gate_weight, kernel_weight, segment_ids, out_grad):
    n_dp = lax.axis_size("dp")
    n_mp = lax.axis_size("mp")
    micro, rows = segment_ids.shape
    full, width = value_weight.shape[1:]
    kcols = kernel_weight.shape[2]
    heads = kcols // KERNEL
    slab = full // n_dp
    span = 2 * width + rows
    vmem = pl.BlockSpec(memory_space=pltpu.VMEM)
    dma = pltpu.SemaphoreType.DMA
    return pl.pallas_call(
        functools.partial(kernel, n_dp, micro),
        out_shape=(
            jax.ShapeDtypeStruct((1, slab, width), F32),
            jax.ShapeDtypeStruct((1, slab, width), F32),
            jax.ShapeDtypeStruct((1, slab, kcols), F32),
        ),
        in_specs=[vmem] * 6,
        out_specs=(vmem, vmem, vmem),
        scratch_shapes=[
            pltpu.VMEM((micro, n_mp, rows, width), BF16),
            pltpu.VMEM((micro, n_mp, rows, width), F32),
            pltpu.VMEM((micro, rows, full), BF16),
            pltpu.VMEM((micro, rows, rows), F32),
            pltpu.VMEM((micro, full, rows), BF16),
            pltpu.VMEM((micro, n_dp, slab, rows), BF16),
            pltpu.VMEM((full, rows), BF16),
            pltpu.VMEM((rows, rows), F32),
            pltpu.VMEM((micro, rows, rows), F32),
            pltpu.VMEM((micro, rows, width), F32),
            pltpu.VMEM((micro, rows, width), F32),
            pltpu.VMEM((micro, rows, width), BF16),
            pltpu.VMEM((micro, heads, rows, rows), F32),
            pltpu.VMEM((micro, heads, rows, rows), BF16),
            pltpu.VMEM((micro, rows, width), BF16),
            pltpu.VMEM((micro, rows, width), BF16),
            pltpu.VMEM((micro, rows, width), BF16),
            pltpu.VMEM((micro, n_dp, rows, span), BF16),
            pltpu.VMEM((micro, n_mp, rows, width), BF16),
            pltpu.VMEM((micro, 3, rows, width), BF16),
            pltpu.VMEM((micro, 8, rows), F32),
            pltpu.VMEM((micro, 3, 8, rows), F32),
            pltpu.VMEM((slab, span), F32),
            dma((micro, 3)),
            dma((micro, 3)),
            dma((micro,)),
            dma((micro,)),
            dma((micro, n_dp)),
            dma((micro, n_dp)),
            dma((micro, n_dp)),
            dma((micro, n_dp)),
            dma((micro, n_dp)),
            dma((micro, 3)),
            dma((micro, 3)),
            dma((micro, 3)),
            dma((micro, 3)),
            dma((micro,)),
            dma((micro,)),
        ],
        compiler_params=pltpu.CompilerParams(
            collective_id=0, has_side_effects=True, vmem_limit_bytes=50 * 1024 * 1024
        ),
    )(source_rows, value_weight, gate_weight, kernel_weight, segment_ids, out_grad)


def solution(mesh):
    in_specs = (
        P("dp", "mp"),
        P("section", None, "mp"),
        P("section", None, "mp"),
        P("section", None, "mp"),
        P("dp", None),
        P("dp", "mp"),
    )
    out_specs = (P("section", "dp", "mp"), P("section", "dp", "mp"), P("section", "dp", "mp"))
    return jax.shard_map(shards, mesh=mesh, in_specs=in_specs, out_specs=out_specs, check_vma=False)
```

time: 362 us -> 72.9 us (0.20)
  waiting for transfers between devices: 179 us -> 0 us
  Pallas kernels: 0 us -> 64.3 us
  other arithmetic: 47.1 us -> 0 us
  matrix products: 38.4 us -> 0 us
  local copies, waits for them, and re-layouts: 42.7 us -> 7.68 us
  blocking collectives: 18.8 us -> 0 us
  starting transfers between devices: 18 us -> 0 us
  between operations: 15.2 us -> 0.65 us
    psum x3 -> x0, waiting for transfers between devices: 134 us -> none  [backward_tick(): lax.psum(grad_part.astype(jnp.bfloat16), 'mp').astype(jnp.float32)]
    pallas_call x0 -> x1, Pallas kernels: none -> 64.3 us  [shards(): pl.pallas_call(functools.partial(kernel, n_dp, micro), out_shape=(jax.Sha...]
    dot_general x32 -> x0, matrix products: 38.4 us -> none  [the longest x4 6.34 us: forward_pieces(): jnp.dot(normed_b, w_kernel, preferred_element_type=jnp.float32)]
    reduce_scatter x1 -> x0, waiting for transfers between devices: 31.9 us -> none  [shards(): lax.psum_scatter(grads.astype(jnp.bfloat16), 'dp', scatter_dimension=0, t...]
    all_gather x3 -> x0, blocking collectives: 18.8 us -> none  [forward_tick(): full_rows = lax.all_gather(own_rows, 'mp', axis=1, tiled=True)]
    ppermute x6 -> x0, starting transfers between devices: 18 us -> none  [from_behind(): lax.ppermute(value, axis, [(source, source + steps) for source in range(i...]
    sub x2 -> x0, other arithmetic: 14.8 us -> none  [layer_backward(): grad_taps - jnp.sum(taps * grad_taps, axis=-1, keepdims=True)]
    ppermute x6 -> x0, waiting for transfers between devices: 12.7 us -> none  [from_behind(): lax.ppermute(value, axis, [(source, source + steps) for source in range(i...]
  transfers between devices with their start and end apart: 10 -> 0, of which waited for: 10 -> 0; matrix products, arithmetic and copies ran while one was open for 2% -> 0% of each run, Pallas kernels for 0% -> 0%
where the time goes in v1:
time: 72.9 us; the launch traced here: 72.6 us
  Pallas kernels  64.3 us (88%)
  local copies, waits for them, and re-layouts  7.68 us (11%)
    pallas_call x1, Pallas kernels, shards(): pl.pallas_call(functools.partial(kernel, n_dp, micro), out_shape=(jax.Sha...  64.3 us
    unnamed x14, local copies, waits for them, and re-layouts  6.92 us

profile of v1, /device:TPU:0, one launch (start us, length us, event | category | flops | bytes accessed | tf_op | source)
XLA Modules:
  0.0 72.6 jit_solution(640534891599018369)
XLA Ops:
  0.6 0.0 copy-start
  0.6 1.0 %copy-done = bf16[1,1024,256]{2,1,0:T(8,128)(2,1)S(1)} copy-done((bf16[1,1024,256]{2,1,0:T(8,128)(2,1)S(1)}, bf16[1,1024,256]{2,1,0:T(8,128)(2,1)}, u32[]{:S(2)}) %copy-start) | copy-done | bytes 524312
  1.7 0.0 copy-start.1
  1.7 1.0 %copy-done.1 = bf16[1,1024,256]{2,1,0:T(8,128)(2,1)S(1)} copy-done((bf16[1,1024,256]{2,1,0:T(8,128)(2,1)S(1)}, bf16[1,1024,256]{2,1,0:T(8,128)(2,1)}, u32[]{:S(2)}) %copy-start.1) | copy-done | bytes 524312
  2.7 0.0 copy-start.2
  2.7 0.9 %copy-done.2 = bf16[1,1024,124]{2,1,0:T(8,128)(2,1)S(1)} copy-done((bf16[1,1024,124]{2,1,0:T(8,128)(2,1)S(1)}, bf16[1,1024,124]{2,1,0:T(8,128)(2,1)}, u32[]{:S(2)}) %copy-start.2) | copy-done | bytes 253976
  3.7 0.0 copy-start.3
  3.7 0.9 %copy-done.3 = bf16[256,256]{1,0:T(8,128)(2,1)S(1)} copy-done((bf16[256,256]{1,0:T(8,128)(2,1)S(1)}, bf16[256,256]{1,0:T(8,128)(2,1)}, u32[]{:S(2)}) %copy-start.3) | copy-done | bytes 131096
  4.6 0.0 copy-start.4
  4.6 0.9 %copy-done.4 = bf16[256,256]{1,0:T(8,128)(2,1)S(1)} copy-done((bf16[256,256]{1,0:T(8,128)(2,1)S(1)}, bf16[256,256]{1,0:T(8,128)(2,1)}, u32[]{:S(2)}) %copy-start.4) | copy-done | bytes 131096
  5.5 0.0 copy-start.5
  5.5 0.7 copy-done.5
  6.2 64.3 %shard_map.85 = (f32[1,256,256]{2,1,0:T(8,128)S(1)}, f32[1,256,256]{2,1,0:T(8,128)S(1)}, f32[1,256,124]{2,1,0:T(8,128)S(1)}) custom-call(bf16[256,256]{1,0:T(8,128)(2,1)S(1)} %copy-done.3, bf16[1,1024,256]{2,1,0:T(8,128)(2,1)S(1)} %copy-done, bf16[1,1024,256]{2,1,0:T(8,128)(2,1)S(1)} %copy-done.1, bf16[1,1024,124]{2,1,0:T(8,128)(2,1)S(1)} %copy-done.2, ...), custom_call_target="tpu_custom_call" | custom-call | tf_op jit(solution)/shard_map/pallas_call | solution.py:462
  70.5 0.8 %copy.9 = f32[1,256,124]{1,0,2:T(1,128)} copy(f32[1,256,124]{2,1,0:T(8,128)S(1)} %get-tuple-element.5) | data formatting | bytes 253952 | tf_op jit(solution)/shard_map/pallas_call | solution.py:462
  71.2 0.7 copy.12
  71.9 0.7 copy.13
Async XLA Ops:
  0.6 1.0 %copy-start = (bf16[1,1024,256]{2,1,0:T(8,128)(2,1)S(1)}, bf16[1,1024,256]{2,1,0:T(8,128)(2,1)}, u32[]{:S(2)}) copy-start(bf16[1,1024,256]{2,1,0:T(8,128)(2,1)} %wv_ref.1) | copy-start | bytes 1572868
  1.7 1.0 %copy-start.1 = (bf16[1,1024,256]{2,1,0:T(8,128)(2,1)S(1)}, bf16[1,1024,256]{2,1,0:T(8,128)(2,1)}, u32[]{:S(2)}) copy-start(bf16[1,1024,256]{2,1,0:T(8,128)(2,1)} %wg_ref.1) | copy-start | bytes 1572868
  2.7 0.9 %copy-start.2 = (bf16[1,1024,124]{2,1,0:T(8,128)(2,1)S(1)}, bf16[1,1024,124]{2,1,0:T(8,128)(2,1)}, u32[]{:S(2)}) copy-start(bf16[1,1024,124]{2,1,0:T(8,128)(2,1)} %wk_ref.1) | copy-start | bytes 761860
  3.7 0.9 %copy-start.3 = (bf16[256,256]{1,0:T(8,128)(2,1)S(1)}, bf16[256,256]{1,0:T(8,128)(2,1)}, u32[]{:S(2)}) copy-start(bf16[256,256]{1,0:T(8,128)(2,1)} %src_ref.1) | copy-start | bytes 393220
  4.6 0.9 %copy-start.4 = (bf16[256,256]{1,0:T(8,128)(2,1)S(1)}, bf16[256,256]{1,0:T(8,128)(2,1)}, u32[]{:S(2)}) copy-start(bf16[256,256]{1,0:T(8,128)(2,1)} %og_ref.1) | copy-start | bytes 393220
  5.5 0.7 copy-start.5

commit v2 on v1

--- a/solution.py
+++ b/solution.py
@@ -47,14 +47,18 @@
     n_dp,
     micro,
     src_ref,
+    wv_hbm,
+    wg_hbm,
+    wk_hbm,
+    seg_hbm,
+    og_ref,
+    vout_ref,
+    gout_ref,
+    kout_ref,
     wv_ref,
     wg_ref,
     wk_ref,
     seg_ref,
-    og_ref,
-    vout_ref,
-    gout_ref,
-    kout_ref,
     xall,
     nf,
     nb,
@@ -69,10 +73,12 @@
     gateds,
     tps,
     bds,
+    bdts,
     hs,
     gbuf,
     gs,
-    terms,
+    pairs,
+    tails,
     rs_buf,
     rs_in,
     st_buf,
@@ -93,6 +99,7 @@
     st_recv,
     g_send,
     g_recv,
+    load_sem,
 ):
     d = lax.axis_index("dp")
     s = lax.axis_index("section")
@@ -103,9 +110,8 @@
     partners = (near, across, corner)
     other = {"section": 1 - s}
     rows = seg_ref.shape[1]
-    width = wv_ref.shape[2]
-    full = wv_ref.shape[1]
-    kcols = wk_ref.shape[2]
+    full, width = wv_ref.shape
+    kcols = wk_ref.shape[1]
     heads = kcols // KERNEL
     n_mp = full // width
     slab = full // n_dp
@@ -131,23 +137,43 @@
 
     lax.fori_loop(1, n_dp, greet, 0)
 
+    loads = [
+        pltpu.make_async_copy(src, dst, load_sem.at[i])
+        for i, (src, dst) in enumerate(
+            (
+                (seg_hbm, seg_ref),
+                (wk_hbm.at[0], wk_ref),
+                (wv_hbm.at[0], wv_ref),
+                (wg_hbm.at[0], wg_ref),
+            )
+        )
+    ]
+
+    def own_load(mb, source, target):
+        piece = source.at[pl.ds(mb * rows, rows), :]
+        return pltpu.make_async_copy(piece, target, load_sem.at[len(loads) + mb])
+
     @pl.when(s == 0)
     def _():
         for mb in micros:
-            xall[mb, m] = src_ref[mb * rows : (mb + 1) * rows, :]
+            own_load(mb, src_ref, xall.at[mb, m]).start()
+
+    for load in loads:
+        load.start()
 
     @pl.when(s == 1)
     def _():
         for mb in micros:
-            gbuf[mb] = og_ref[mb * rows : (mb + 1) * rows, :]
+            own_load(mb, og_ref, gbuf.at[mb]).start()
 
     pl.semaphore_wait(barrier, 4 + n_dp - 1)
 
-    def gather_copy(mb, rel):
+    def gather_copy(mb, rel, first=False):
         block = (m, m, across)[rel]
         target = (near, across, near)[rel]
+        source = src_ref.at[pl.ds(mb * rows, rows), :] if first else xall.at[mb, block]
         return remote(
-            xall.at[mb, block],
+            source,
             xall.at[mb, block],
             ag_send.at[mb, rel],
             ag_recv.at[mb, rel],
@@ -173,30 +199,44 @@
     @pl.when(s == 0)
     def _():
         for mb in micros:
-            gather_copy(mb, 1).start()
-            gather_copy(mb, 0).start()
+            gather_copy(mb, 1, True).start()
+            gather_copy(mb, 0, True).start()
 
     wkp[...] = jnp.zeros_like(wkp)
-    wkp[:, :kcols] = wk_ref[0]
-    lgs[...] = jnp.zeros_like(lgs)
     acc[...] = jnp.zeros_like(acc)
+    loads[0].wait()
     for mb in micros:
         across_seg = jnp.broadcast_to(seg_ref[mb : mb + 1, :].astype(F32), (rows, rows))
         down_seg = jnp.transpose(across_seg)
         same = (across_seg == down_seg) & (offset >= 0) & (offset < KERNEL)
         masks[mb] = jnp.where(same, 1.0, 0.0)
-
-    def forward(mb):
-        @pl.when(s == 1)
-        def _():
-            h_copy(mb).wait_recv()
-            gather_copy(mb, 1).start()
-            gather_copy(mb, 0).start()
-
+    loads[1].wait()
+    wkp[:, :kcols] = wk_ref[...]
+    loads[2].wait()
+    loads[3].wait()
+
+    @pl.when(s == 0)
+    def _():
+        for mb in micros:
+            own_load(mb, src_ref, xall.at[mb, m]).wait()
+
+    @pl.when(s == 1)
+    def _():
+        for mb in micros:
+            own_load(mb, og_ref, gbuf.at[mb]).wait()
+
+    def gather_start(mb):
+        h_copy(mb).wait_recv()
+        gather_copy(mb, 1).start()
+        gather_copy(mb, 0).start()
+
+    def gather_finish(mb):
         gather_wait(mb, 1)
         gather_copy(mb, 2).start()
         gather_wait(mb, 0)
         gather_wait(mb, 2)
+
+    def forward(mb):
         blocks = [xall[mb, j].astype(F32) for j in range(n_mp)]
         mean = sum(jnp.sum(b, axis=1, keepdims=True) for b in blocks) / full
         centred = [b - mean for b in blocks]
@@ -209,9 +249,9 @@
             nb[mb, :, j * width : (j + 1) * width] = normed.astype(BF16)
         normed_b = nb[mb]
         lgs[...] = dot(normed_b, wkp[...])
-        value = dot(normed_b, wv_ref[0])
-        sig = jax.nn.sigmoid(dot(normed_b, wg_ref[0]))
-        vs[mb] = value
+        value = dot(normed_b, wv_ref[...])
+        sig = jax.nn.sigmoid(dot(normed_b, wg_ref[...]))
+        vs[mb] = value * (1.0 - sig)
         sigs[mb] = sig
         gateds[mb] = (value * sig).astype(BF16)
         logits = lgs[...]
@@ -224,20 +264,23 @@
             tps[mb, h] = taps
             bds[mb, h] = jnp.where(in_band, taps, 0.0).astype(BF16)
 
-        @pl.when(s == 0)
-        def _():
-            for p in range(heads // 2):
-                cols = slice(p * rows, (p + 1) * rows)
-                pair = gateds[mb, :, cols]
-                mixed = jnp.where(
-                    low_half, dot(bds[mb, 2 * p], pair), dot(bds[mb, 2 * p + 1], pair)
-                )
-                own = src_ref[mb * rows : (mb + 1) * rows, cols].astype(F32)
-                hs[mb, :, cols] = (own + mixed).astype(BF16)
-            h_copy(mb).start()
-
-        for j in range(n_mp):
-            nt_full[mb, j * width : (j + 1) * width, :] = jnp.transpose(nf[mb, j]).astype(BF16)
+    def mix(mb):
+        for p in range(heads // 2):
+            cols = slice(p * rows, (p + 1) * rows)
+            pair = gateds[mb, :, cols]
+            mixed = jnp.where(
+                low_half, dot(bds[mb, 2 * p], pair), dot(bds[mb, 2 * p + 1], pair)
+            )
+            own = xall[mb, m, :, cols].astype(F32)
+            hs[mb, :, cols] = (own + mixed).astype(BF16)
+        h_copy(mb).start()
+
+    def turn(mb):
+        for h in range(heads):
+            bdts[mb, h] = jnp.transpose(bds[mb, h])
+
+    def share_normed(mb):
+        nt_full[mb] = jnp.transpose(nb[mb])
 
         def share(i, carry):
             k = lax.rem(d + i, n_dp)
@@ -256,46 +299,50 @@
             {"dp": k},
         )
 
-    def ring_copy(mb, k, step):
+    chunks = range(heads // 2 + 1)
+
+    def chunk(mb, k, c):
+        return tails.at[mb, k] if c == heads // 2 else pairs.at[mb, k, c]
+
+    def ring_copy(mb, k, c, step):
         sems = right_send if step == 1 else left_send
         return remote(
-            terms.at[mb, k],
-            terms.at[mb, k],
-            sems.at[mb, k],
-            ring_recv.at[mb, k],
+            chunk(mb, k, c),
+            chunk(mb, k, c),
+            sems.at[mb, k, c],
+            ring_recv.at[mb, k, c],
             {"dp": d + step},
         )
 
-    def ring_start(mb, k_right, k_left):
+    def ring_start(mb, k_right, k_left, c):
         @pl.when((d + 1 < n_dp) & (k_right >= 0))
         def _():
-            ring_copy(mb, k_right, 1).start()
+            ring_copy(mb, k_right, c, 1).start()
 
         @pl.when((d > 0) & (k_left < n_dp))
         def _():
-            ring_copy(mb, k_left, -1).start()
-
-    def backward(mb):
-        @pl.when(s == 0)
-        def _():
-            g_copy(mb).wait_recv()
-
+            ring_copy(mb, k_left, c, -1).start()
+
+    def backward(mb, eager):
         in_band = masks[mb] > 0.0
+        for p in range(heads // 2):
+            cols = slice(p * rows, (p + 1) * rows)
+            grad_pair = gbuf[mb, :, cols]
+            grad_gated = jnp.where(
+                low_half,
+                dot(bdts[mb, 2 * p], grad_pair),
+                dot(bdts[mb, 2 * p + 1], grad_pair),
+            )
+            grad_value = grad_gated * sigs[mb, :, cols]
+            pairs[mb, d, p, :, :rows] = grad_value.astype(BF16)
+            pairs[mb, d, p, :, rows:] = (grad_value * vs[mb, :, cols]).astype(BF16)
+            if eager:
+                ring_start(mb, d, d, p)
         grad_logits = jnp.zeros((rows, rows), F32)
         for p in range(heads // 2):
             cols = slice(p * rows, (p + 1) * rows)
             grad_pair = gbuf[mb, :, cols]
             gated_pair = gateds[mb, :, cols]
-            grad_gated = jnp.where(
-                low_half,
-                dot_tn(bds[mb, 2 * p], grad_pair),
-                dot_tn(bds[mb, 2 * p + 1], grad_pair),
-            )
-            sig = sigs[mb, :, cols]
-            grad_value = grad_gated * sig
-            terms[mb, d, :, cols] = grad_value.astype(BF16)
-            grad_gate = grad_value * vs[mb, :, cols] * (1.0 - sig)
-            terms[mb, d, :, width + p * rows : width + (p + 1) * rows] = grad_gate.astype(BF16)
             for half in range(2):
                 h = 2 * p + half
                 keep = low_half if half == 0 else ~low_half
@@ -306,33 +353,31 @@
                 skewed = (taps * (grad_taps - inner)).astype(BF16)
                 shift = (KERNEL // 2 + KERNEL * h + 1) % rows
                 grad_logits = grad_logits + skew(dot(flip, skewed), shift)
-        terms[mb, d, :, 2 * width :] = dot(flip, grad_logits.astype(BF16)).astype(BF16)
-
-        @pl.when(s == 0)
-        def _():
-            ring_start(mb, d, d)
-
-        @pl.when(s == 1)
-        def _():
-            grad_value = terms[mb, d, :, :width]
-            grad_gate = terms[mb, d, :, width : 2 * width]
-            grad_log = terms[mb, d, :, 2 * width :]
-            first = jnp.zeros((rows, 1), F32)
-            second = jnp.zeros((rows, 1), F32)
-            for j in range(n_mp):
-                span = slice(j * width, (j + 1) * width)
-                part = dot_nt(grad_value, wv_ref[0, span, :])
-                part = part + dot_nt(grad_gate, wg_ref[0, span, :])
-                part = part + dot_nt(grad_log, wkp[span, :])
-                rs_buf[mb, j] = part.astype(BF16)
-                first = first + jnp.sum(part, axis=1, keepdims=True)
-                second = second + jnp.sum(part * nf[mb, j], axis=1, keepdims=True)
-            both = jnp.transpose(jnp.where(lanes == 0, first, second))
-            st_buf[mb] = both[:8]
-            for rel in range(3):
-                rs_copy(mb, rel).start()
-                st_copy(mb, rel).start()
-            ring_start(mb, d, d)
+        tails[mb, d] = dot(flip, grad_logits.astype(BF16)).astype(BF16)
+        if eager:
+            ring_start(mb, d, d, heads // 2)
+
+    def scatter(mb):
+        grad_value = jnp.concatenate([pairs[mb, d, p, :, :rows] for p in range(heads // 2)], axis=1)
+        grad_gate = jnp.concatenate([pairs[mb, d, p, :, rows:] for p in range(heads // 2)], axis=1)
+        grad_log = tails[mb, d]
+        first = jnp.zeros((rows, 1), F32)
+        second = jnp.zeros((rows, 1), F32)
+        for j in range(n_mp):
+            span = slice(j * width, (j + 1) * width)
+            part = dot_nt(grad_value, wv_ref[span, :])
+            part = part + dot_nt(grad_gate, wg_ref[span, :])
+            part = part + dot_nt(grad_log, wkp[span, :])
+            rs_buf[mb, j] = part.astype(BF16)
+            first = first + jnp.sum(part, axis=1, keepdims=True)
+            second = second + jnp.sum(part * nf[mb, j], axis=1, keepdims=True)
+        both = jnp.transpose(jnp.where(lanes == 0, first, second))
+        st_buf[mb] = both[:8]
+        for rel in (1, 2, 0):
+            rs_copy(mb, rel).start()
+            st_copy(mb, rel).start()
+        for c in chunks:
+            ring_start(mb, d, d, c)
 
     def rs_copy(mb, rel):
         return remote(
@@ -366,54 +411,92 @@
         gs[mb] = (gbuf[mb].astype(F32) + grad).astype(BF16)
         g_copy(mb).start()
 
-    for mb in micros:
-        forward(mb)
-    for mb in micros:
-        backward(mb)
-
-        @pl.when(s == 1)
-        def _():
-            finish(mb)
-
     def accumulate(mb, k):
-        acc[...] += dot(nt_all[mb, k], terms[mb, k])
-
-    for mb in micros:
-        accumulate(mb, d)
-
-    def ring_step(i, carry):
-        for mb in micros:
-            left, right = d - i, d + i
+        for c in range(heads // 2):
+            acc[c] += dot(nt_all[mb, k], pairs[mb, k, c])
+        acc[heads // 2, :, :rows] += dot(nt_all[mb, k], tails[mb, k])
+
+    def ring_step(mb, i):
+        left, right = d - i, d + i
+        for c in chunks:
 
             @pl.when(left >= 0)
             def _():
-                ring_copy(mb, left, -1).wait_recv()
+                ring_copy(mb, left, c, -1).wait_recv()
 
             @pl.when(right < n_dp)
             def _():
-                ring_copy(mb, right, 1).wait_recv()
-
-            ring_start(mb, left, right)
-            for k, there in ((left, left >= 0), (right, right < n_dp)):
-
-                @pl.when(there)
-                def _():
-                    remote(
-                        nt_all.at[mb, k],
-                        nt_all.at[mb, k],
-                        nt_send.at[mb, k],
-                        nt_recv.at[mb, k],
-                        {"dp": k},
-                    ).wait_recv()
-                    accumulate(mb, k)
-
+                ring_copy(mb, right, c, 1).wait_recv()
+
+            ring_start(mb, left, right, c)
+        for k, there in ((left, left >= 0), (right, right < n_dp)):
+
+            @pl.when(there)
+            def _():
+                remote(
+                    nt_all.at[mb, k],
+                    nt_all.at[mb, k],
+                    nt_send.at[mb, k],
+                    nt_recv.at[mb, k],
+                    {"dp": k},
+                ).wait_recv()
+                accumulate(mb, k)
+
+    last = micro - 1
+
+    @pl.when(s == 0)
+    def _():
+        for mb in micros:
+            gather_finish(mb)
+            forward(mb)
+            mix(mb)
+        for mb in micros:
+            share_normed(mb)
+            turn(mb)
+        for mb in micros:
+            g_copy(mb).wait_recv()
+            backward(mb, True)
+            accumulate(mb, d)
+            if mb < last:
+                ring_step(mb, 1)
+
+    @pl.when(s == 1)
+    def _():
+        gather_start(0)
+        for mb in micros:
+            gather_finish(mb)
+            forward(mb)
+            turn(mb)
+            if mb < last:
+                gather_start(mb + 1)
+            if mb > 0:
+                finish(mb - 1)
+            backward(mb, False)
+            scatter(mb)
+            share_normed(mb)
+        accumulate(0, d)
+        finish(last)
+        for mb in range(1, micro):
+            accumulate(mb, d)
+        for mb in range(last):
+            ring_step(mb, 1)
+
+    def ring_round(i, carry):
+        for mb in range(last):
+
+            @pl.when(i + 1 < n_dp)
+            def _():
+                ring_step(mb, i + 1)
+
+        ring_step(last, i)
         return carry
 
-    lax.fori_loop(1, n_dp, ring_step, 0)
-
-    vout_ref[0] = acc[:, :width]
-    gout_ref[0] = acc[:, width : 2 * width]
-    kout_ref[0] = acc[:, 2 * width : 2 * width + kcols]
+    lax.fori_loop(1, n_dp, ring_round, 0)
+
+    for p in range(heads // 2):
+        vout_ref[0, :, p * rows : (p + 1) * rows] = acc[p, :, :rows]
+        gout_ref[0, :, p * rows : (p + 1) * rows] = acc[p, :, rows:]
+    kout_ref[0] = acc[heads // 2, :, :kcols]
 
     for mb in micros:
         for rel in range(3):
@@ -437,11 +520,13 @@
 
             @pl.when((d + 1 < n_dp) & (d - i >= 0))
             def _():
-                ring_copy(mb, d - i, 1).wait_send()
+                for c in chunks:
+                    ring_copy(mb, d - i, c, 1).wait_send()
 
             @pl.when((d > 0) & (d + i < n_dp))
             def _():
-                ring_copy(mb, d + i, -1).wait_send()
+                for c in chunks:
+                    ring_copy(mb, d + i, c, -1).wait_send()
 
             return carry
 
@@ -456,8 +541,9 @@
     kcols = kernel_weight.shape[2]
     heads = kcols // KERNEL
     slab = full // n_dp
-    span = 2 * width + rows
+    groups = heads // 2
     vmem = pl.BlockSpec(memory_space=pltpu.VMEM)
+    hbm = pl.BlockSpec(memory_space=pltpu.HBM)
     dma = pltpu.SemaphoreType.DMA
     return pl.pallas_call(
         functools.partial(kernel, n_dp, micro),
@@ -466,9 +552,13 @@
             jax.ShapeDtypeStruct((1, slab, width), F32),
             jax.ShapeDtypeStruct((1, slab, kcols), F32),
         ),
-        in_specs=[vmem] * 6,
+        in_specs=[hbm] * 6,
         out_specs=(vmem, vmem, vmem),
         scratch_shapes=[
+            pltpu.VMEM((full, width), BF16),
+            pltpu.VMEM((full, width), BF16),
+            pltpu.VMEM((full, kcols), BF16),
+            pltpu.VMEM((micro, rows), jnp.int32),
             pltpu.VMEM((micro, n_mp, rows, width), BF16),
             pltpu.VMEM((micro, n_mp, rows, width), F32),
             pltpu.VMEM((micro, rows, full), BF16),
@@ -483,30 +573,33 @@
             pltpu.VMEM((micro, rows, width), BF16),
             pltpu.VMEM((micro, heads, rows, rows), F32),
             pltpu.VMEM((micro, heads, rows, rows), BF16),
+            pltpu.VMEM((micro, heads, rows, rows), BF16),
             pltpu.VMEM((micro, rows, width), BF16),
             pltpu.VMEM((micro, rows, width), BF16),
             pltpu.VMEM((micro, rows, width), BF16),
-            pltpu.VMEM((micro, n_dp, rows, span), BF16),
+            pltpu.VMEM((micro, n_dp, groups, rows, width), BF16),
+            pltpu.VMEM((micro, n_dp, rows, rows), BF16),
             pltpu.VMEM((micro, n_mp, rows, width), BF16),
             pltpu.VMEM((micro, 3, rows, width), BF16),
             pltpu.VMEM((micro, 8, rows), F32),
             pltpu.VMEM((micro, 3, 8, rows), F32),
-            pltpu.VMEM((slab, span), F32),
+            pltpu.VMEM((groups + 1, slab, width), F32),
             dma((micro, 3)),
             dma((micro, 3)),
             dma((micro,)),
             dma((micro,)),
             dma((micro, n_dp)),
             dma((micro, n_dp)),
-            dma((micro, n_dp)),
-            dma((micro, n_dp)),
-            dma((micro, n_dp)),
+            dma((micro, n_dp, groups + 1)),
+            dma((micro, n_dp, groups + 1)),
+            dma((micro, n_dp, groups + 1)),
             dma((micro, 3)),
             dma((micro, 3)),
             dma((micro, 3)),
             dma((micro, 3)),
             dma((micro,)),
             dma((micro,)),
+            dma((4 + micro,)),
         ],
         compiler_params=pltpu.CompilerParams(
             collective_id=0, has_side_effects=True, vmem_limit_bytes=50 * 1024 * 1024

time: 72.9 us -> 62.6 us (0.86)
  Pallas kernels: 64.3 us -> 53.7 us
    pallas_call x1, Pallas kernels: 64.3 us -> 53.7 us  [shards(): pl.pallas_call(functools.partial(kernel, n_dp, micro), out_shape=(jax.Sha...]
where the time goes in v2:
time: 62.6 us; the launch traced here: 62 us
  Pallas kernels  53.7 us (86%)
  local copies, waits for them, and re-layouts  7.68 us (12%)
  between operations  0.65 us (1%)
    pallas_call x1, Pallas kernels, shards(): pl.pallas_call(functools.partial(kernel, n_dp, micro), out_shape=(jax.Sha...  53.7 us
    unnamed x14, local copies, waits for them, and re-layouts  6.92 us

profile of v2, /device:TPU:0, one launch (start us, length us, event | category | flops | bytes accessed | tf_op | source)
XLA Modules:
  0.0 62.0 jit_solution(15092709707364933544)
XLA Ops:
  0.6 0.0 copy-start
  0.6 1.0 %copy-done = bf16[1,1024,256]{2,1,0:T(8,128)(2,1)S(1)} copy-done((bf16[1,1024,256]{2,1,0:T(8,128)(2,1)S(1)}, bf16[1,1024,256]{2,1,0:T(8,128)(2,1)}, u32[]{:S(2)}) %copy-start) | copy-done | bytes 524312
  1.7 0.0 copy-start.1
  1.7 1.0 %copy-done.1 = bf16[1,1024,256]{2,1,0:T(8,128)(2,1)S(1)} copy-done((bf16[1,1024,256]{2,1,0:T(8,128)(2,1)S(1)}, bf16[1,1024,256]{2,1,0:T(8,128)(2,1)}, u32[]{:S(2)}) %copy-start.1) | copy-done | bytes 524312
  2.7 0.0 copy-start.2
  2.7 0.9 %copy-done.2 = bf16[1,1024,124]{2,1,0:T(8,128)(2,1)S(1)} copy-done((bf16[1,1024,124]{2,1,0:T(8,128)(2,1)S(1)}, bf16[1,1024,124]{2,1,0:T(8,128)(2,1)}, u32[]{:S(2)}) %copy-start.2) | copy-done | bytes 253976
  3.7 0.0 copy-start.3
  3.7 0.9 %copy-done.3 = bf16[256,256]{1,0:T(8,128)(2,1)S(1)} copy-done((bf16[256,256]{1,0:T(8,128)(2,1)S(1)}, bf16[256,256]{1,0:T(8,128)(2,1)}, u32[]{:S(2)}) %copy-start.3) | copy-done | bytes 131096
  4.6 0.0 copy-start.4
  4.6 0.9 %copy-done.4 = bf16[256,256]{1,0:T(8,128)(2,1)S(1)} copy-done((bf16[256,256]{1,0:T(8,128)(2,1)S(1)}, bf16[256,256]{1,0:T(8,128)(2,1)}, u32[]{:S(2)}) %copy-start.4) | copy-done | bytes 131096
  5.5 0.0 copy-start.5
  5.5 0.7 %copy-done.5 = s32[2,128]{1,0:T(2,128)S(1)} copy-done((s32[2,128]{1,0:T(2,128)S(1)}, s32[2,128]{1,0:T(2,128)}, u32[]{:S(2)}) %copy-start.5) | copy-done | bytes 1048
  6.2 53.7 %shard_map.85 = (f32[1,256,256]{2,1,0:T(8,128)S(1)}, f32[1,256,256]{2,1,0:T(8,128)S(1)}, f32[1,256,124]{2,1,0:T(8,128)S(1)}) custom-call(bf16[256,256]{1,0:T(8,128)(2,1)S(1)} %copy-done.3, bf16[1,1024,256]{2,1,0:T(8,128)(2,1)S(1)} %copy-done, bf16[1,1024,256]{2,1,0:T(8,128)(2,1)S(1)} %copy-done.1, bf16[1,1024,124]{2,1,0:T(8,128)(2,1)S(1)} %copy-done.2, ...), custom_call_target="tpu_custom_call" | custom-call | tf_op jit(solution)/shard_map/pallas_call | solution.py:548
  59.8 0.8 %copy.9 = f32[1,256,124]{1,0,2:T(1,128)} copy(f32[1,256,124]{2,1,0:T(8,128)S(1)} %get-tuple-element.5) | data formatting | bytes 253952 | tf_op jit(solution)/shard_map/pallas_call | solution.py:548
  60.6 0.7 %copy.12 = f32[1,256,256]{2,1,0:T(8,128)} copy(f32[1,256,256]{2,1,0:T(8,128)S(1)} %get-tuple-element.9) | data formatting | bytes 524288
  61.3 0.7 %copy.13 = f32[1,256,256]{2,1,0:T(8,128)} copy(f32[1,256,256]{2,1,0:T(8,128)S(1)} %get-tuple-element.10) | data formatting | bytes 524288
Async XLA Ops:
  0.6 1.0 %copy-start = (bf16[1,1024,256]{2,1,0:T(8,128)(2,1)S(1)}, bf16[1,1024,256]{2,1,0:T(8,128)(2,1)}, u32[]{:S(2)}) copy-start(bf16[1,1024,256]{2,1,0:T(8,128)(2,1)} %wv_hbm.1) | copy-start | bytes 1572868
  1.7 1.0 %copy-start.1 = (bf16[1,1024,256]{2,1,0:T(8,128)(2,1)S(1)}, bf16[1,1024,256]{2,1,0:T(8,128)(2,1)}, u32[]{:S(2)}) copy-start(bf16[1,1024,256]{2,1,0:T(8,128)(2,1)} %wg_hbm.1) | copy-start | bytes 1572868
  2.7 0.9 %copy-start.2 = (bf16[1,1024,124]{2,1,0:T(8,128)(2,1)S(1)}, bf16[1,1024,124]{2,1,0:T(8,128)(2,1)}, u32[]{:S(2)}) copy-start(bf16[1,1024,124]{2,1,0:T(8,128)(2,1)} %wk_hbm.1) | copy-start | bytes 761860
  3.7 0.9 %copy-start.3 = (bf16[256,256]{1,0:T(8,128)(2,1)S(1)}, bf16[256,256]{1,0:T(8,128)(2,1)}, u32[]{:S(2)}) copy-start(bf16[256,256]{1,0:T(8,128)(2,1)} %src_ref.1) | copy-start | bytes 393220
  4.6 0.9 %copy-start.4 = (bf16[256,256]{1,0:T(8,128)(2,1)S(1)}, bf16[256,256]{1,0:T(8,128)(2,1)}, u32[]{:S(2)}) copy-start(bf16[256,256]{1,0:T(8,128)(2,1)} %og_ref.1) | copy-start | bytes 393220
  5.5 0.7 %copy-start.5 = (s32[2,128]{1,0:T(2,128)S(1)}, s32[2,128]{1,0:T(2,128)}, u32[]{:S(2)}) copy-start(s32[2,128]{1,0:T(2,128)} %seg_hbm.1) | copy-start | bytes 3076

commit v3 on v2

--- a/solution.py
+++ b/solution.py
@@ -496,7 +496,8 @@
     for p in range(heads // 2):
         vout_ref[0, :, p * rows : (p + 1) * rows] = acc[p, :, :rows]
         gout_ref[0, :, p * rows : (p + 1) * rows] = acc[p, :, rows:]
-    kout_ref[0] = acc[heads // 2, :, :kcols]
+    turned = jnp.transpose(acc[heads // 2, :, :rows])
+    kout_ref[:, 0, :] = turned[:kcols]
 
     for mb in micros:
         for rel in range(3):
@@ -531,6 +532,15 @@
             return carry
 
         lax.fori_loop(0, n_dp, drain, 0)
+
+
+def deliver(*refs):
+    sems = refs[6]
+    copies = [pltpu.make_async_copy(refs[i], refs[3 + i], sems.at[i]) for i in range(3)]
+    for copy in copies:
+        copy.start()
+    for copy in copies:
+        copy.wait()
 
 
 def shards(source_rows, value_weight, gate_weight, kernel_weight, segment_ids, out_grad):
@@ -545,12 +555,12 @@
     vmem = pl.BlockSpec(memory_space=pltpu.VMEM)
     hbm = pl.BlockSpec(memory_space=pltpu.HBM)
     dma = pltpu.SemaphoreType.DMA
-    return pl.pallas_call(
+    shares = pl.pallas_call(
         functools.partial(kernel, n_dp, micro),
         out_shape=(
             jax.ShapeDtypeStruct((1, slab, width), F32),
             jax.ShapeDtypeStruct((1, slab, width), F32),
-            jax.ShapeDtypeStruct((1, slab, kcols), F32),
+            jax.ShapeDtypeStruct((kcols, 1, slab), F32),
         ),
         in_specs=[hbm] * 6,
         out_specs=(vmem, vmem, vmem),
@@ -602,9 +612,17 @@
             dma((4 + micro,)),
         ],
         compiler_params=pltpu.CompilerParams(
-            collective_id=0, has_side_effects=True, vmem_limit_bytes=50 * 1024 * 1024
+            collective_id=0, has_side_effects=True, vmem_limit_bytes=62 * 1024 * 1024
         ),
     )(source_rows, value_weight, gate_weight, kernel_weight, segment_ids, out_grad)
+    value_share, gate_share, kernel_share = pl.pallas_call(
+        deliver,
+        out_shape=tuple(jax.ShapeDtypeStruct(x.shape, x.dtype) for x in shares),
+        in_specs=[hbm] * 3,
+        out_specs=(hbm,) * 3,
+        scratch_shapes=[dma((3,))],
+    )(*shares)
+    return (value_share, gate_share, jnp.transpose(kernel_share, (1, 2, 0)))
 
 
 def solution(mesh):

time: 62.6 us -> 76.8 us (1.23)
  Pallas kernels: 53.7 us -> 75.7 us
  local copies, waits for them, and re-layouts: 7.68 us -> 0 us
    pallas_call x0 -> x1, Pallas kernels: none -> 20.9 us  [shards(): pl.pallas_call(deliver, out_shape=tuple((jax.ShapeDtypeStruct(x.shape, x....]
    unnamed x14 -> x0, local copies, waits for them, and re-layouts: 6.92 us -> none
    pallas_call x1, Pallas kernels: 53.7 us -> 54.8 us  [shards(): pl.pallas_call(functools.partial(kernel, n_dp, micro), out_shape=(jax.Sha...]
where the time goes in v3:
time: 76.8 us; the launch traced here: 76.3 us
  Pallas kernels  75.7 us (99%)
    pallas_call x1, Pallas kernels, shards(): pl.pallas_call(functools.partial(kernel, n_dp, micro), out_shape=(jax.Sha...  54.8 us
    pallas_call x1, Pallas kernels, shards(): pl.pallas_call(deliver, out_shape=tuple((jax.ShapeDtypeStruct(x.shape, x....  20.9 us

profile of v3, /device:TPU:0, one launch (start us, length us, event | category | flops | bytes accessed | tf_op | source)
XLA Modules:
  0.0 76.3 jit_solution(10462356972404433685)
XLA Ops:
  0.6 54.8 %shard_map.85 = (f32[1,256,256]{2,1,0:T(8,128)}, f32[1,256,256]{2,1,0:T(8,128)}, f32[124,1,256]{2,1,0:T(1,128)}) custom-call(bf16[256,256]{1,0:T(8,128)(2,1)} %src_ref.1, bf16[1,1024,256]{2,1,0:T(8,128)(2,1)} %wv_hbm.1, bf16[1,1024,256]{2,1,0:T(8,128)(2,1)} %wg_hbm.1, bf16[1,1024,124]{2,1,0:T(8,128)(2,1)} %wk_hbm.1, s32[2,128]{1,0:T(2,128)} %seg_hbm.1, ...), custom_call_target="tpu_custom_call" | custom-call | tf_op jit(solution)/shard_map/pallas_call | solution.py:558
  55.5 20.9 %shard_map.86 = (f32[1,256,256]{2,1,0:T(8,128)}, f32[1,256,256]{2,1,0:T(8,128)}, f32[124,1,256]{2,1,0:T(1,128)}) custom-call(f32[1,256,256]{2,1,0:T(8,128)} %get-tuple-element.9.refs_0_, f32[1,256,256]{2,1,0:T(8,128)} %get-tuple-element.10.refs_1_, f32[124,1,256]{2,1,0:T(1,128)} %get-tuple-element.11.refs_2_), custom_call_target="tpu_custom_call" | custom-call | tf_op jit(solution)/shard_map/pallas_call | solution.py:618

commit v4 on v3

--- a/solution.py
+++ b/solution.py
@@ -535,12 +535,16 @@
 
 
 def deliver(*refs):
-    sems = refs[6]
-    copies = [pltpu.make_async_copy(refs[i], refs[3 + i], sems.at[i]) for i in range(3)]
+    sources, targets, stages, sems = refs[:3], refs[3:6], refs[6:9], refs[9]
+    copies = [pltpu.make_async_copy(sources[i], stages[i], sems.at[i]) for i in range(3)]
     for copy in copies:
         copy.start()
-    for copy in copies:
+    leaving = [pltpu.make_async_copy(stages[i], targets[i], sems.at[3 + i]) for i in range(3)]
+    for copy, leave in zip(copies, leaving):
         copy.wait()
+        leave.start()
+    for leave in leaving:
+        leave.wait()
 
 
 def shards(source_rows, value_weight, gate_weight, kernel_weight, segment_ids, out_grad):
@@ -620,7 +624,7 @@
         out_shape=tuple(jax.ShapeDtypeStruct(x.shape, x.dtype) for x in shares),
         in_specs=[hbm] * 3,
         out_specs=(hbm,) * 3,
-        scratch_shapes=[dma((3,))],
+        scratch_shapes=[pltpu.VMEM(x.shape, x.dtype) for x in shares] + [dma((6,))],
     )(*shares)
     return (value_share, gate_share, jnp.transpose(kernel_share, (1, 2, 0)))
 

time: 76.8 us -> 57.7 us (0.75)
  Pallas kernels: 75.7 us -> 56.6 us
    pallas_call x1, Pallas kernels: 20.9 us -> 1.82 us  [shards(): pl.pallas_call(deliver, out_shape=tuple((jax.ShapeDtypeStruct(x.shape, x....]
where the time goes in v4:
time: 57.7 us; the launch traced here: 57.3 us
  Pallas kernels  56.6 us (98%)
  between operations  0.64 us (1%)
    pallas_call x1, Pallas kernels, shards(): pl.pallas_call(functools.partial(kernel, n_dp, micro), out_shape=(jax.Sha...  54.8 us
    pallas_call x1, Pallas kernels, shards(): pl.pallas_call(deliver, out_shape=tuple((jax.ShapeDtypeStruct(x.shape, x....  1.82 us

profile of v4, /device:TPU:0, one launch (start us, length us, event | category | flops | bytes accessed | tf_op | source)
XLA Modules:
  0.0 57.3 jit_solution(2667076747458060174)
XLA Ops:
  0.6 54.8 %shard_map.85 = (f32[1,256,256]{2,1,0:T(8,128)}, f32[1,256,256]{2,1,0:T(8,128)}, f32[124,1,256]{2,1,0:T(1,128)}) custom-call(bf16[256,256]{1,0:T(8,128)(2,1)} %src_ref.1, bf16[1,1024,256]{2,1,0:T(8,128)(2,1)} %wv_hbm.1, bf16[1,1024,256]{2,1,0:T(8,128)(2,1)} %wg_hbm.1, bf16[1,1024,124]{2,1,0:T(8,128)(2,1)} %wk_hbm.1, s32[2,128]{1,0:T(2,128)} %seg_hbm.1, ...), custom_call_target="tpu_custom_call" | custom-call | tf_op jit(solution)/shard_map/pallas_call | solution.py:562
  55.5 1.8 %shard_map.86 = (f32[1,256,256]{2,1,0:T(8,128)}, f32[1,256,256]{2,1,0:T(8,128)}, f32[124,1,256]{2,1,0:T(1,128)}) custom-call(f32[1,256,256]{2,1,0:T(8,128)} %get-tuple-element.9.refs_0_, f32[1,256,256]{2,1,0:T(8,128)} %get-tuple-element.10.refs_1_, f32[124,1,256]{2,1,0:T(1,128)} %get-tuple-element.11.refs_2_), custom_call_target="tpu_custom_call" | custom-call | tf_op jit(solution)/shard_map/pallas_call | solution.py:622

commit v5 on v4

--- a/solution.py
+++ b/solution.py
@@ -411,12 +411,12 @@
         gs[mb] = (gbuf[mb].astype(F32) + grad).astype(BF16)
         g_copy(mb).start()
 
-    def accumulate(mb, k):
+    def accumulate(k):
         for c in range(heads // 2):
-            acc[c] += dot(nt_all[mb, k], pairs[mb, k, c])
-        acc[heads // 2, :, :rows] += dot(nt_all[mb, k], tails[mb, k])
-
-    def ring_step(mb, i):
+            acc[c] += sum(dot(nt_all[mb, k], pairs[mb, k, c]) for mb in micros)
+        acc[heads // 2, :, :rows] += sum(dot(nt_all[mb, k], tails[mb, k]) for mb in micros)
+
+    def ring_forward(mb, i):
         left, right = d - i, d + i
         for c in chunks:
 
@@ -429,18 +429,6 @@
                 ring_copy(mb, right, c, 1).wait_recv()
 
             ring_start(mb, left, right, c)
-        for k, there in ((left, left >= 0), (right, right < n_dp)):
-
-            @pl.when(there)
-            def _():
-                remote(
-                    nt_all.at[mb, k],
-                    nt_all.at[mb, k],
-                    nt_send.at[mb, k],
-                    nt_recv.at[mb, k],
-                    {"dp": k},
-                ).wait_recv()
-                accumulate(mb, k)
 
     last = micro - 1
 
@@ -456,9 +444,8 @@
         for mb in micros:
             g_copy(mb).wait_recv()
             backward(mb, True)
-            accumulate(mb, d)
             if mb < last:
-                ring_step(mb, 1)
+                ring_forward(mb, 1)
 
     @pl.when(s == 1)
     def _():
@@ -474,21 +461,37 @@
             backward(mb, False)
             scatter(mb)
             share_normed(mb)
-        accumulate(0, d)
+        for mb in range(last):
+            ring_forward(mb, 1)
         finish(last)
-        for mb in range(1, micro):
-            accumulate(mb, d)
-        for mb in range(last):
-            ring_step(mb, 1)
 
     def ring_round(i, carry):
         for mb in range(last):
 
             @pl.when(i + 1 < n_dp)
             def _():
-                ring_step(mb, i + 1)
-
-        ring_step(last, i)
+                ring_forward(mb, i + 1)
+
+        ring_forward(last, i)
+
+        @pl.when(i == 1)
+        def _():
+            accumulate(d)
+
+        for k, there in ((d - i, d - i >= 0), (d + i, d + i < n_dp)):
+
+            @pl.when(there)
+            def _():
+                for mb in micros:
+                    remote(
+                        nt_all.at[mb, k],
+                        nt_all.at[mb, k],
+                        nt_send.at[mb, k],
+                        nt_recv.at[mb, k],
+                        {"dp": k},
+                    ).wait_recv()
+                accumulate(k)
+
         return carry
 
     lax.fori_loop(1, n_dp, ring_round, 0)

time: 57.7 us -> 57.8 us (level)
  no operation moved by 1% of the time
where the time goes in v5:
time: 57.8 us; the launch traced here: 57.3 us
  Pallas kernels  56.7 us (98%)
  between operations  0.64 us (1%)
    pallas_call x1, Pallas kernels, shards(): pl.pallas_call(functools.partial(kernel, n_dp, micro), out_shape=(jax.Sha...  54.9 us
    pallas_call x1, Pallas kernels, shards(): pl.pallas_call(deliver, out_shape=tuple((jax.ShapeDtypeStruct(x.shape, x....  1.82 us

profile of v5, /device:TPU:0, one launch (start us, length us, event | category | flops | bytes accessed | tf_op | source)
XLA Modules:
  0.0 57.3 jit_solution(17401004328239955861)
XLA Ops:
  0.6 54.9 %shard_map.85 = (f32[1,256,256]{2,1,0:T(8,128)}, f32[1,256,256]{2,1,0:T(8,128)}, f32[124,1,256]{2,1,0:T(1,128)}) custom-call(bf16[256,256]{1,0:T(8,128)(2,1)} %src_ref.1, bf16[1,1024,256]{2,1,0:T(8,128)(2,1)} %wv_hbm.1, bf16[1,1024,256]{2,1,0:T(8,128)(2,1)} %wg_hbm.1, bf16[1,1024,124]{2,1,0:T(8,128)(2,1)} %wk_hbm.1, s32[2,128]{1,0:T(2,128)} %seg_hbm.1, ...), custom_call_target="tpu_custom_call" | custom-call | tf_op jit(solution)/shard_map/pallas_call | solution.py:565
  55.5 1.8 %shard_map.86 = (f32[1,256,256]{2,1,0:T(8,128)}, f32[1,256,256]{2,1,0:T(8,128)}, f32[124,1,256]{2,1,0:T(1,128)}) custom-call(f32[1,256,256]{2,1,0:T(8,128)} %get-tuple-element.9.refs_0_, f32[1,256,256]{2,1,0:T(8,128)} %get-tuple-element.10.refs_1_, f32[124,1,256]{2,1,0:T(1,128)} %get-tuple-element.11.refs_2_), custom_call_target="tpu_custom_call" | custom-call | tf_op jit(solution)/shard_map/pallas_call | solution.py:625

commit v6 on v5

--- a/solution.py
+++ b/solution.py
@@ -458,9 +458,9 @@
                 gather_start(mb + 1)
             if mb > 0:
                 finish(mb - 1)
+            share_normed(mb)
             backward(mb, False)
             scatter(mb)
-            share_normed(mb)
         for mb in range(last):
             ring_forward(mb, 1)
         finish(last)

time: 57.8 us -> 57.6 us (level)
  no operation moved by 1% of the time
where the time goes in v6:
time: 57.6 us; the launch traced here: 57.5 us
  Pallas kernels  56.8 us (99%)
  between operations  0.64 us (1%)
    pallas_call x1, Pallas kernels, shards(): pl.pallas_call(functools.partial(kernel, n_dp, micro), out_shape=(jax.Sha...  55 us
    pallas_call x1, Pallas kernels, shards(): pl.pallas_call(deliver, out_shape=tuple((jax.ShapeDtypeStruct(x.shape, x....  1.82 us

profile of v6, /device:TPU:0, one launch (start us, length us, event | category | flops | bytes accessed | tf_op | source)
XLA Modules:
  0.0 57.5 jit_solution(18359304122523403881)
XLA Ops:
  0.6 55.0 %shard_map.85 = (f32[1,256,256]{2,1,0:T(8,128)}, f32[1,256,256]{2,1,0:T(8,128)}, f32[124,1,256]{2,1,0:T(1,128)}) custom-call(bf16[256,256]{1,0:T(8,128)(2,1)} %src_ref.1, bf16[1,1024,256]{2,1,0:T(8,128)(2,1)} %wv_hbm.1, bf16[1,1024,256]{2,1,0:T(8,128)(2,1)} %wg_hbm.1, bf16[1,1024,124]{2,1,0:T(8,128)(2,1)} %wk_hbm.1, s32[2,128]{1,0:T(2,128)} %seg_hbm.1, ...), custom_call_target="tpu_custom_call" | custom-call | tf_op jit(solution)/shard_map/pallas_call | solution.py:565
  55.7 1.8 %shard_map.86 = (f32[1,256,256]{2,1,0:T(8,128)}, f32[1,256,256]{2,1,0:T(8,128)}, f32[124,1,256]{2,1,0:T(1,128)}) custom-call(f32[1,256,256]{2,1,0:T(8,128)} %get-tuple-element.9.refs_0_, f32[1,256,256]{2,1,0:T(8,128)} %get-tuple-element.10.refs_1_, f32[124,1,256]{2,1,0:T(1,128)} %get-tuple-element.11.refs_2_), custom_call_target="tpu_custom_call" | custom-call | tf_op jit(solution)/shard_map/pallas_call | solution.py:625
